TPU v7x, 512 devices: a whole 4x4x16 slice. The times are simulated.
512 devices in a mesh: seq: 16 (over x, y), exp: 32 (over z, core).
Axes of the slice: x: 4, y: 4, z: 16, core: 2. Of those that a mesh axis runs over, the one named last changes fastest.
Arguments:
- residual: bfloat16 [2048, 2, 3072], P(('seq', 'exp')), may hold values from -6 to 6
- queries: bfloat16 [2, 2048, 4096], P(None, 'seq', 'exp'), may hold values from -6 to 6
- key_vecs: bfloat16 [2, 2048, 4096], P(None, 'seq', 'exp'), may hold values from -0.52734375 to 0.52734375
- value_vecs: bfloat16 [2, 2048, 4096], P(None, 'seq', 'exp'), may hold values from -6 to 6
- log_decay: float32 [2, 32, 2048], P(None, 'exp', 'seq'), may hold values from -2 to 0
- head_gain: float32 [4096], P('exp'), may hold values from 0.1 to 1.9
- out_proj: bfloat16 [4096, 3072], P('exp'), may hold values from -0.09375 to 0.09375
- norm_gain: float32 [3072], replicated, may hold values from 0.1 to 1.9
- routes: int32 [2048, 2, 2], replicated, may hold values from 0 to 31, all different within a row; in each aligned block of 256 rows (0 to 255, 256 to 511, ..., all dimensions but the last counted through in order) at most 32 rows name the same one
- route_weight: float32 [2048, 2, 2], replicated, may hold values from 0.1 to 1
- w_gate: bfloat16 [32, 4608, 3072], P('exp', 'seq'), may hold values from -0.109375 to 0.109375
- w_up: bfloat16 [32, 4608, 3072], P('exp', 'seq'), may hold values from -0.109375 to 0.109375
Outputs:
- attn_out: float32 [2048, 2, 3072], P(('seq', 'exp'))
- expert_hidden: float32 [32, 4608, 512], P('exp', 'seq')
Inputs may be any that keep to these rules, and one draw needn't show every extreme that they name: Each aligned block of 256 rows of routes (positions c * 128 .. (c + 1) * 128 - 1 of both sequences) names one expert at most 32 times, a bound that some block reaches; the 2 entries of a row differ.
All inputs are finite; a program needn't handle non-finite values.
Results may differ from a plain program's by a relative error of at most 0.0052.
Values may be sent and summed in bfloat16 or wider, within the bound.
A program may use at most 64 MiB of HBM per device.

v0:
```python
import jax
import jax.numpy as jnp
from jax import lax
from jax.sharding import PartitionSpec as P

PRECISE = lax.Precision.HIGHEST


def passed_along(block, axis, distance):
    devices = range(lax.axis_size(axis))
    route = [(i - distance, i) for i in devices if i - distance in devices]
    return lax.ppermute(block, axis, route)


def row_norm(values_in, gain_vec):
    meansq = jnp.mean(values_in * values_in, axis=-1, keepdims=True)
    return values_in * lax.rsqrt(meansq + 1e-06) * gain_vec


def per_device(
    residual,
    queries,
    key_vecs,
    value_vecs,
    log_decay,
    head_gain,
    out_proj,
    norm_gain,
    routes,
    route_weight,
    w_gate,
    w_up,
):
    seq_total, group_len, feat_width = queries.shape
    head_count = log_decay.shape[1]
    head_size = feat_width // head_count
    query_t = queries.reshape(seq_total, group_len, head_count, head_size)
    key_t = key_vecs.reshape(seq_total, group_len, head_count, head_size)
    value_t = value_vecs.reshape(seq_total, group_len, head_count, head_size).astype(jnp.float32)
    running = jnp.cumsum(log_decay, axis=-1)
    causal_mask = jnp.tril(jnp.ones((group_len, group_len), dtype=bool))
    spread_log = running[..., :, None] - running[..., None, :]
    decay_mat = jnp.where(causal_mask, jnp.exp(jnp.where(causal_mask, spread_log, 0.0)), 0.0)
    scores = (
        jnp.einsum("bthc,bjhc->bhtj", query_t, key_t, preferred_element_type=jnp.float32)
        * decay_mat
    )
    inner_part = jnp.einsum("bhtj,bjhd->bhtd", scores, value_t, precision=PRECISE)
    block_total = running[..., -1]
    tail_decay = jnp.exp(block_total[..., None] - running)
    weighted_keys = key_t.astype(jnp.float32) * jnp.swapaxes(tail_decay, 1, 2)[..., None]
    fresh_state = jnp.einsum("bjhc,bjhd->bhcd", weighted_keys, value_t, precision=PRECISE)

    def advance(turn_index, incoming):
        outgoing = jnp.exp(block_total)[..., None, None] * incoming + fresh_state
        return passed_along(outgoing, "seq", 1)

    incoming = lax.fori_loop(0, lax.axis_size("seq") - 1, advance, jnp.zeros_like(fresh_state))
    outer_part = jnp.exp(running)[..., None] * jnp.einsum(
        "bthc,bhcd->bhtd", query_t.astype(jnp.float32), incoming, precision=PRECISE
    )
    gain_grid = head_gain.reshape(head_count, head_size)[None, :, None, :]
    normed_heads = row_norm(inner_part + outer_part, gain_grid)
    attention = (
        jnp.transpose(normed_heads, (2, 0, 1, 3))
        .reshape(group_len, seq_total, feat_width)
        .astype(jnp.bfloat16)
    )
    own_rows = residual.shape[0]
    model_width = residual.shape[2]
    offset = lax.axis_index("exp") * own_rows
    seq_count = lax.axis_size("seq")
    owner_count = lax.axis_size("exp")
    row_count = group_len * seq_total
    top_count = routes.shape[-1]
    route_blocks = routes.reshape(seq_count, row_count, top_count)
    weight_blocks = route_weight.reshape(seq_count, row_count, top_count)
    placed = lax.dynamic_update_slice_in_dim(
        jnp.zeros((group_len, seq_total, model_width), jnp.float32),
        residual.astype(jnp.float32),
        offset,
        0,
    )
    mixed_all = lax.psum(
        jnp.einsum("tbk,kd->tbd", attention, out_proj, preferred_element_type=jnp.float32) + placed,
        "exp",
    )
    normed_all = row_norm(mixed_all, norm_gain).astype(jnp.bfloat16).reshape(row_count, model_width)
    mixed_rows = lax.dynamic_slice_in_dim(mixed_all, offset, own_rows, 0)
    capacity = 8 * group_len // owner_count
    expert_id = lax.axis_index("exp")
    route_hits = route_blocks == expert_id
    chosen = jnp.any(route_hits, axis=-1)
    token_weight = jnp.sum(jnp.where(route_hits, weight_blocks, 0.0), axis=-1)
    slot_rank = jnp.cumsum(chosen.astype(jnp.int32), axis=1) - 1
    slot_ids = jnp.arange(capacity, dtype=jnp.int32)
    pick_table = ((slot_rank[:, None, :] == slot_ids[None, :, None]) & chosen[:, None, :]).astype(
        jnp.float32
    )
    slot_weight = jnp.einsum("csj,cj->cs", pick_table, token_weight, precision=PRECISE).reshape(-1)
    own_picks = lax.dynamic_index_in_dim(pick_table, lax.axis_index("seq"), 0, keepdims=False)
    slot_rows = jnp.dot(
        own_picks.astype(jnp.bfloat16), normed_all, preferred_element_type=jnp.float32
    ).astype(jnp.bfloat16)
    row_piece = lax.all_gather(slot_rows, "seq", axis=0, tiled=True)
    gate_val = lax.dot_general(
        w_gate[0], row_piece, (((1,), (1,)), ((), ())), preferred_element_type=jnp.float32
    )
    up_val = lax.dot_general(
        w_up[0], row_piece, (((1,), (1,)), ((), ())), preferred_element_type=jnp.float32
    )
    hidden = slot_weight[None, :] * jax.nn.silu(gate_val) * up_val
    return (mixed_rows, hidden[None])


def solution(mesh):
    placed = (
        P(("seq", "exp"), None, None),
        P(None, "seq", "exp"),
        P(None, "seq", "exp"),
        P(None, "seq", "exp"),
        P(None, "exp", "seq"),
        P("exp"),
        P("exp", None),
        P(),
        P(),
        P(),
        P("exp", "seq", None),
        P("exp", "seq", None),
    )
    return jax.shard_map(
        per_device,
        mesh=mesh,
        in_specs=placed,
        out_specs=(P(("seq", "exp"), None, None), P("exp", "seq", None)),
        check_vma=False,
    )
```

profile of v0, /device:TPU:1, one launch (start us, length us, event | category | flops | bytes accessed | tf_op | source)
XLA Modules:
  0.0 460.5 jit_solution(3259821568363661606)
XLA Ops:
  7.3 1.4 reduce_window_sum.28
  8.7 0.2 slice_reduce_fusion.1
  8.9 1.2 convolution_bitcast_fusion
  10.2 1.0 convolution_multiply_fusion.1
  11.3 110.8 %while.12 = (s32[]{:T(128)}, f32[2,1,128,128]{3,2,1,0:T(8,128)S(1)}, f32[2,1,1,1]{0,3,2,1:T(1,128)S(1)}, f32[2,1,128,128]{3,2,1,0:T(8,128)S(1)}, s32[]{:T(128)}) while((s32[]{:T(128)}, f32[2,1,128,128]{3,2,1,0:T(8,128)S(1)}, f32[2,1,1,1]{0,3,2,1:T(1,128)S(1)}, f32[2,1,128,128]{3,2,1,0:T(8,128)S(1)}, s32[]{:T(128)}) %tuple.45), condition=%wide.region_2.3_spmd, body=%wide.region_1.2_spmd.sunk | while | flops 65538 | bytes 917613 | solution.py:58
  11.3 0.1 multiply_add_fusion.2
  11.4 4.0 collective-permute-start
  15.4 1.9 collective-permute-done
  17.3 0.1 multiply_add_fusion.2
  17.4 3.8 collective-permute-start
  21.2 1.9 collective-permute-done
  23.2 3.8 collective-permute-start
  27.0 3.0 collective-permute-done
  30.0 3.8 collective-permute-start
  33.9 2.5 collective-permute-done
  36.4 4.1 collective-permute-start
  40.6 1.9 collective-permute-done
  42.6 5.1 %collective-permute-start = (f32[2,1,128,128]{3,2,1,0:T(8,128)S(1)}, f32[2,1,128,128]{3,2,1,0:T(8,128)S(1)}, u32[]{:S(2)}, u32[]{:S(2)}) collective-permute-start(f32[2,1,128,128]{3,2,1,0:T(8,128)S(1)} %multiply_add_fusion.2), channel_id=1, source_target_pairs={{0,32},{32,64},{64,96},{96,128},{128,160},{160,192},{192,224},{224... | collective-permute-start | bytes 393224 | tf_op jit(solution)/shard_map/while/body/eval_jaxpr/ppermute | solution.py:12
  47.7 1.9 collective-permute-done
  49.7 6.0 %collective-permute-start = (f32[2,1,128,128]{3,2,1,0:T(8,128)S(1)}, f32[2,1,128,128]{3,2,1,0:T(8,128)S(1)}, u32[]{:S(2)}, u32[]{:S(2)}) collective-permute-start(f32[2,1,128,128]{3,2,1,0:T(8,128)S(1)} %multiply_add_fusion.2), channel_id=1, source_target_pairs={{0,32},{32,64},{64,96},{96,128},{128,160},{160,192},{192,224},{224... | collective-permute-start | bytes 393224 | tf_op jit(solution)/shard_map/while/body/eval_jaxpr/ppermute | solution.py:12
  55.8 2.7 collective-permute-done
  58.6 5.3 %collective-permute-start = (f32[2,1,128,128]{3,2,1,0:T(8,128)S(1)}, f32[2,1,128,128]{3,2,1,0:T(8,128)S(1)}, u32[]{:S(2)}, u32[]{:S(2)}) collective-permute-start(f32[2,1,128,128]{3,2,1,0:T(8,128)S(1)} %multiply_add_fusion.2), channel_id=1, source_target_pairs={{0,32},{32,64},{64,96},{96,128},{128,160},{160,192},{192,224},{224... | collective-permute-start | bytes 393224 | tf_op jit(solution)/shard_map/while/body/eval_jaxpr/ppermute | solution.py:12
  63.9 2.5 collective-permute-done
  66.4 5.0 %collective-permute-start = (f32[2,1,128,128]{3,2,1,0:T(8,128)S(1)}, f32[2,1,128,128]{3,2,1,0:T(8,128)S(1)}, u32[]{:S(2)}, u32[]{:S(2)}) collective-permute-start(f32[2,1,128,128]{3,2,1,0:T(8,128)S(1)} %multiply_add_fusion.2), channel_id=1, source_target_pairs={{0,32},{32,64},{64,96},{96,128},{128,160},{160,192},{192,224},{224... | collective-permute-start | bytes 393224 | tf_op jit(solution)/shard_map/while/body/eval_jaxpr/ppermute | solution.py:12
  71.4 1.9 collective-permute-done
  73.4 6.8 %collective-permute-start = (f32[2,1,128,128]{3,2,1,0:T(8,128)S(1)}, f32[2,1,128,128]{3,2,1,0:T(8,128)S(1)}, u32[]{:S(2)}, u32[]{:S(2)}) collective-permute-start(f32[2,1,128,128]{3,2,1,0:T(8,128)S(1)} %multiply_add_fusion.2), channel_id=1, source_target_pairs={{0,32},{32,64},{64,96},{96,128},{128,160},{160,192},{192,224},{224... | collective-permute-start | bytes 393224 | tf_op jit(solution)/shard_map/while/body/eval_jaxpr/ppermute | solution.py:12
  80.3 1.9 collective-permute-done
  82.3 6.0 %collective-permute-start = (f32[2,1,128,128]{3,2,1,0:T(8,128)S(1)}, f32[2,1,128,128]{3,2,1,0:T(8,128)S(1)}, u32[]{:S(2)}, u32[]{:S(2)}) collective-permute-start(f32[2,1,128,128]{3,2,1,0:T(8,128)S(1)} %multiply_add_fusion.2), channel_id=1, source_target_pairs={{0,32},{32,64},{64,96},{96,128},{128,160},{160,192},{192,224},{224... | collective-permute-start | bytes 393224 | tf_op jit(solution)/shard_map/while/body/eval_jaxpr/ppermute | solution.py:12
  88.3 1.9 collective-permute-done
  90.3 5.8 %collective-permute-start = (f32[2,1,128,128]{3,2,1,0:T(8,128)S(1)}, f32[2,1,128,128]{3,2,1,0:T(8,128)S(1)}, u32[]{:S(2)}, u32[]{:S(2)}) collective-permute-start(f32[2,1,128,128]{3,2,1,0:T(8,128)S(1)} %multiply_add_fusion.2), channel_id=1, source_target_pairs={{0,32},{32,64},{64,96},{96,128},{128,160},{160,192},{192,224},{224... | collective-permute-start | bytes 393224 | tf_op jit(solution)/shard_map/while/body/eval_jaxpr/ppermute | solution.py:12
  96.1 1.9 collective-permute-done
  98.1 6.2 %collective-permute-start = (f32[2,1,128,128]{3,2,1,0:T(8,128)S(1)}, f32[2,1,128,128]{3,2,1,0:T(8,128)S(1)}, u32[]{:S(2)}, u32[]{:S(2)}) collective-permute-start(f32[2,1,128,128]{3,2,1,0:T(8,128)S(1)} %multiply_add_fusion.2), channel_id=1, source_target_pairs={{0,32},{32,64},{64,96},{96,128},{128,160},{160,192},{192,224},{224... | collective-permute-start | bytes 393224 | tf_op jit(solution)/shard_map/while/body/eval_jaxpr/ppermute | solution.py:12
  104.3 1.9 collective-permute-done
  106.3 5.9 %collective-permute-start = (f32[2,1,128,128]{3,2,1,0:T(8,128)S(1)}, f32[2,1,128,128]{3,2,1,0:T(8,128)S(1)}, u32[]{:S(2)}, u32[]{:S(2)}) collective-permute-start(f32[2,1,128,128]{3,2,1,0:T(8,128)S(1)} %multiply_add_fusion.2), channel_id=1, source_target_pairs={{0,32},{32,64},{64,96},{96,128},{128,160},{160,192},{192,224},{224... | collective-permute-start | bytes 393224 | tf_op jit(solution)/shard_map/while/body/eval_jaxpr/ppermute | solution.py:12
  112.2 1.9 collective-permute-done
  114.2 5.9 %collective-permute-start = (f32[2,1,128,128]{3,2,1,0:T(8,128)S(1)}, f32[2,1,128,128]{3,2,1,0:T(8,128)S(1)}, u32[]{:S(2)}, u32[]{:S(2)}) collective-permute-start(f32[2,1,128,128]{3,2,1,0:T(8,128)S(1)} %multiply_add_fusion.2), channel_id=1, source_target_pairs={{0,32},{32,64},{64,96},{96,128},{128,160},{160,192},{192,224},{224... | collective-permute-start | bytes 393224 | tf_op jit(solution)/shard_map/while/body/eval_jaxpr/ppermute | solution.py:12
  120.1 1.9 collective-permute-done
  122.1 1.1 fusion.16
  123.2 0.3 multiply_reduce_fusion.1
  123.6 2.4 fusion.17
  125.9 1.6 add_dynamic-update-slice_fusion
  127.7 0.5 copy.40
  128.2 0.4 copy.37
  128.6 0.6 reshape.171
  129.2 0.6 reduce-window.6
  129.8 0.2 slice_reduce_fusion
  130.0 0.7 and.12
  130.7 0.1 fusion.19
  130.8 244.0 %all-reduce.2.cloned.1.call-done = f32[128,2,3072]{2,0,1:T(8,128)} async-done(((f32[128,2,3072]{2,0,1:T(8,128)}), f32[128,2,3072]{2,0,1:T(8,128)}) %all-reduce.2.cloned.1.call-update) | async-done | bytes 3145744 | tf_op jit(solution)/shard_map/psum | solution.py:84
  374.8 2.3 multiply_reduce_fusion
  377.2 0.5 copy-done.1
  377.7 0.5 multiply_convert_fusion
  378.1 2.8 copy.42
  380.9 3.6 reshape.170
  384.5 1.1 convolution_convert_fusion
  385.7 0.4 copy.41
  386.1 0.6 reshape.176
  386.7 0.3 fusion.33
  387.0 0.1 mul.112
  387.1 1.0 constant_dynamic-slice_fusion
  388.1 0.7 copy.43
  388.8 59.7 %all-gather.2.cloned.1.call-done = bf16[512,3072]{1,0:T(8,128)(2,1)} async-done(((bf16[32,3072]{1,0:T(8,128)(2,1)}), bf16[512,3072]{1,0:T(8,128)(2,1)}) %all-gather.2.cloned.1.call-update) | async-done | bytes 3145744 | tf_op jit(solution)/shard_map/all_gather | solution.py:105
  448.5 3.1 fusion.4
  451.7 2.0 fusion.13
  (50 shorter events, 1.6 us)
Async XLA Ops:
  7.2 441.3 %copy-start = (bf16[1,288,3072]{2,1,0:T(8,128)(2,1)S(1)}, bf16[1,288,3072]{2,1,0:T(8,128)(2,1)}, u32[]{:S(2)}) copy-start(bf16[1,288,3072]{2,1,0:T(8,128)(2,1)} %param.24) | copy-start | bytes 5308420
  7.2 116.0 %copy-start.3 = (bf16[2,128,128]{2,1,0:T(8,128)(2,1)S(1)}, bf16[2,128,128]{2,1,0:T(8,128)(2,1)}, u32[]{:S(2)}) copy-start(bf16[2,128,128]{2,1,0:T(8,128)(2,1)} %param.17) | copy-start | bytes 196612
  7.2 116.3 %copy-start.2 = (bf16[128,3072]{1,0:T(8,128)(2,1)S(1)}, bf16[128,3072]{1,0:T(8,128)(2,1)}, u32[]{:S(2)}) copy-start(bf16[128,3072]{1,0:T(8,128)(2,1)} %param.20) | copy-start | bytes 2359300
  7.2 116.3 %copy-start.8 = (f32[128]{0:T(128)S(1)}, f32[128]{0:T(128)}, u32[]{:S(2)}) copy-start(f32[128]{0:T(128)} %param.19) | copy-start | bytes 1540
  7.2 367.6 %all-reduce.2.cloned.1.call-start = ((), (), s32[]{:S(2)}) async-start(), calls=%async_computation | async-start | bytes 6291456 | tf_op jit(solution)/shard_map/psum | solution.py:84
  11.2 114.7 %copy-start.5 = (bf16[4,2,3072]{2,1,0:T(2,128)(2,1)S(1)}, bf16[4,2,3072]{2,1,0:T(2,128)(2,1)}, u32[]{:S(2)}) copy-start(bf16[4,2,3072]{2,1,0:T(2,128)(2,1)} %param.14) | copy-start | bytes 147460
  11.4 6.0 %collective-permute-start = (f32[2,1,128,128]{3,2,1,0:T(8,128)S(1)}, f32[2,1,128,128]{3,2,1,0:T(8,128)S(1)}, u32[]{:S(2)}, u32[]{:S(2)}) collective-permute-start(f32[2,1,128,128]{3,2,1,0:T(8,128)S(1)} %multiply_add_fusion.2), channel_id=1, source_target_pairs={{0,32},{32,64},{64,96},{96,128},{128,160},{160,192},{192,224},{224... | collective-permute-start | bytes 393224 | tf_op jit(solution)/shard_map/while/body/eval_jaxpr/ppermute | solution.py:12
  17.4 5.7 %collective-permute-start = (f32[2,1,128,128]{3,2,1,0:T(8,128)S(1)}, f32[2,1,128,128]{3,2,1,0:T(8,128)S(1)}, u32[]{:S(2)}, u32[]{:S(2)}) collective-permute-start(f32[2,1,128,128]{3,2,1,0:T(8,128)S(1)} %multiply_add_fusion.2), channel_id=1, source_target_pairs={{0,32},{32,64},{64,96},{96,128},{128,160},{160,192},{192,224},{224... | collective-permute-start | bytes 393224 | tf_op jit(solution)/shard_map/while/body/eval_jaxpr/ppermute | solution.py:12
  23.2 6.8 %collective-permute-start = (f32[2,1,128,128]{3,2,1,0:T(8,128)S(1)}, f32[2,1,128,128]{3,2,1,0:T(8,128)S(1)}, u32[]{:S(2)}, u32[]{:S(2)}) collective-permute-start(f32[2,1,128,128]{3,2,1,0:T(8,128)S(1)} %multiply_add_fusion.2), channel_id=1, source_target_pairs={{0,32},{32,64},{64,96},{96,128},{128,160},{160,192},{192,224},{224... | collective-permute-start | bytes 393224 | tf_op jit(solution)/shard_map/while/body/eval_jaxpr/ppermute | solution.py:12
  30.0 6.3 %collective-permute-start = (f32[2,1,128,128]{3,2,1,0:T(8,128)S(1)}, f32[2,1,128,128]{3,2,1,0:T(8,128)S(1)}, u32[]{:S(2)}, u32[]{:S(2)}) collective-permute-start(f32[2,1,128,128]{3,2,1,0:T(8,128)S(1)} %multiply_add_fusion.2), channel_id=1, source_target_pairs={{0,32},{32,64},{64,96},{96,128},{128,160},{160,192},{192,224},{224... | collective-permute-start | bytes 393224 | tf_op jit(solution)/shard_map/while/body/eval_jaxpr/ppermute | solution.py:12
  36.4 6.0 %collective-permute-start = (f32[2,1,128,128]{3,2,1,0:T(8,128)S(1)}, f32[2,1,128,128]{3,2,1,0:T(8,128)S(1)}, u32[]{:S(2)}, u32[]{:S(2)}) collective-permute-start(f32[2,1,128,128]{3,2,1,0:T(8,128)S(1)} %multiply_add_fusion.2), channel_id=1, source_target_pairs={{0,32},{32,64},{64,96},{96,128},{128,160},{160,192},{192,224},{224... | collective-permute-start | bytes 393224 | tf_op jit(solution)/shard_map/while/body/eval_jaxpr/ppermute | solution.py:12
  42.6 7.0 %collective-permute-start = (f32[2,1,128,128]{3,2,1,0:T(8,128)S(1)}, f32[2,1,128,128]{3,2,1,0:T(8,128)S(1)}, u32[]{:S(2)}, u32[]{:S(2)}) collective-permute-start(f32[2,1,128,128]{3,2,1,0:T(8,128)S(1)} %multiply_add_fusion.2), channel_id=1, source_target_pairs={{0,32},{32,64},{64,96},{96,128},{128,160},{160,192},{192,224},{224... | collective-permute-start | bytes 393224 | tf_op jit(solution)/shard_map/while/body/eval_jaxpr/ppermute | solution.py:12
  49.7 8.8 %collective-permute-start = (f32[2,1,128,128]{3,2,1,0:T(8,128)S(1)}, f32[2,1,128,128]{3,2,1,0:T(8,128)S(1)}, u32[]{:S(2)}, u32[]{:S(2)}) collective-permute-start(f32[2,1,128,128]{3,2,1,0:T(8,128)S(1)} %multiply_add_fusion.2), channel_id=1, source_target_pairs={{0,32},{32,64},{64,96},{96,128},{128,160},{160,192},{192,224},{224... | collective-permute-start | bytes 393224 | tf_op jit(solution)/shard_map/while/body/eval_jaxpr/ppermute | solution.py:12
  58.6 7.8 %collective-permute-start = (f32[2,1,128,128]{3,2,1,0:T(8,128)S(1)}, f32[2,1,128,128]{3,2,1,0:T(8,128)S(1)}, u32[]{:S(2)}, u32[]{:S(2)}) collective-permute-start(f32[2,1,128,128]{3,2,1,0:T(8,128)S(1)} %multiply_add_fusion.2), channel_id=1, source_target_pairs={{0,32},{32,64},{64,96},{96,128},{128,160},{160,192},{192,224},{224... | collective-permute-start | bytes 393224 | tf_op jit(solution)/shard_map/while/body/eval_jaxpr/ppermute | solution.py:12
  66.4 6.9 %collective-permute-start = (f32[2,1,128,128]{3,2,1,0:T(8,128)S(1)}, f32[2,1,128,128]{3,2,1,0:T(8,128)S(1)}, u32[]{:S(2)}, u32[]{:S(2)}) collective-permute-start(f32[2,1,128,128]{3,2,1,0:T(8,128)S(1)} %multiply_add_fusion.2), channel_id=1, source_target_pairs={{0,32},{32,64},{64,96},{96,128},{128,160},{160,192},{192,224},{224... | collective-permute-start | bytes 393224 | tf_op jit(solution)/shard_map/while/body/eval_jaxpr/ppermute | solution.py:12
  73.4 8.8 %collective-permute-start = (f32[2,1,128,128]{3,2,1,0:T(8,128)S(1)}, f32[2,1,128,128]{3,2,1,0:T(8,128)S(1)}, u32[]{:S(2)}, u32[]{:S(2)}) collective-permute-start(f32[2,1,128,128]{3,2,1,0:T(8,128)S(1)} %multiply_add_fusion.2), channel_id=1, source_target_pairs={{0,32},{32,64},{64,96},{96,128},{128,160},{160,192},{192,224},{224... | collective-permute-start | bytes 393224 | tf_op jit(solution)/shard_map/while/body/eval_jaxpr/ppermute | solution.py:12
  82.3 7.9 %collective-permute-start = (f32[2,1,128,128]{3,2,1,0:T(8,128)S(1)}, f32[2,1,128,128]{3,2,1,0:T(8,128)S(1)}, u32[]{:S(2)}, u32[]{:S(2)}) collective-permute-start(f32[2,1,128,128]{3,2,1,0:T(8,128)S(1)} %multiply_add_fusion.2), channel_id=1, source_target_pairs={{0,32},{32,64},{64,96},{96,128},{128,160},{160,192},{192,224},{224... | collective-permute-start | bytes 393224 | tf_op jit(solution)/shard_map/while/body/eval_jaxpr/ppermute | solution.py:12
  90.3 7.7 %collective-permute-start = (f32[2,1,128,128]{3,2,1,0:T(8,128)S(1)}, f32[2,1,128,128]{3,2,1,0:T(8,128)S(1)}, u32[]{:S(2)}, u32[]{:S(2)}) collective-permute-start(f32[2,1,128,128]{3,2,1,0:T(8,128)S(1)} %multiply_add_fusion.2), channel_id=1, source_target_pairs={{0,32},{32,64},{64,96},{96,128},{128,160},{160,192},{192,224},{224... | collective-permute-start | bytes 393224 | tf_op jit(solution)/shard_map/while/body/eval_jaxpr/ppermute | solution.py:12
  98.1 8.2 %collective-permute-start = (f32[2,1,128,128]{3,2,1,0:T(8,128)S(1)}, f32[2,1,128,128]{3,2,1,0:T(8,128)S(1)}, u32[]{:S(2)}, u32[]{:S(2)}) collective-permute-start(f32[2,1,128,128]{3,2,1,0:T(8,128)S(1)} %multiply_add_fusion.2), channel_id=1, source_target_pairs={{0,32},{32,64},{64,96},{96,128},{128,160},{160,192},{192,224},{224... | collective-permute-start | bytes 393224 | tf_op jit(solution)/shard_map/while/body/eval_jaxpr/ppermute | solution.py:12
  106.3 7.8 %collective-permute-start = (f32[2,1,128,128]{3,2,1,0:T(8,128)S(1)}, f32[2,1,128,128]{3,2,1,0:T(8,128)S(1)}, u32[]{:S(2)}, u32[]{:S(2)}) collective-permute-start(f32[2,1,128,128]{3,2,1,0:T(8,128)S(1)} %multiply_add_fusion.2), channel_id=1, source_target_pairs={{0,32},{32,64},{64,96},{96,128},{128,160},{160,192},{192,224},{224... | collective-permute-start | bytes 393224 | tf_op jit(solution)/shard_map/while/body/eval_jaxpr/ppermute | solution.py:12
  114.2 7.8 %collective-permute-start = (f32[2,1,128,128]{3,2,1,0:T(8,128)S(1)}, f32[2,1,128,128]{3,2,1,0:T(8,128)S(1)}, u32[]{:S(2)}, u32[]{:S(2)}) collective-permute-start(f32[2,1,128,128]{3,2,1,0:T(8,128)S(1)} %multiply_add_fusion.2), channel_id=1, source_target_pairs={{0,32},{32,64},{64,96},{96,128},{128,160},{160,192},{192,224},{224... | collective-permute-start | bytes 393224 | tf_op jit(solution)/shard_map/while/body/eval_jaxpr/ppermute | solution.py:12
  123.5 4.1 copy-start.4
  127.5 249.6 %copy-start.7 = (f32[3072]{0:T(1024)S(1)}, f32[3072]{0:T(1024)}, u32[]{:S(2)}) copy-start(f32[3072]{0:T(1024)} %param.21) | copy-start | bytes 36868
  127.6 320.9 %all-gather.2.cloned.1.call-start = ((), (), s32[]{:S(2)}) async-start(), calls=%async_computation.1 | async-start | bytes 3342336 | tf_op jit(solution)/shard_map/all_gather | solution.py:105
  374.8 2.8 copy-start.1
  380.9 4.8 %copy-start.6 = (f32[2048,2,2]{0,2,1:T(2,128)S(1)}, f32[2048,2,2]{0,2,1:T(2,128)}, u32[]{:S(2)}) copy-start(f32[2048,2,2]{0,2,1:T(2,128)} %param.23) | copy-start | bytes 98308
  388.8 62.8 %copy-start.10 = (bf16[1,288,3072]{2,1,0:T(8,128)(2,1)S(1)}, bf16[1,288,3072]{2,1,0:T(8,128)(2,1)}, u32[]{:S(2)}) copy-start(bf16[1,288,3072]{2,1,0:T(8,128)(2,1)} %param.25) | copy-start | bytes 5308420
  448.5 3.2 copy-start.9
Sparse Core Ops, SparseCore 0:
  127.7 247.1 all-reduce.1
  385.8 62.6 all-gather.1
where the time goes:
time: 461 us; the launch traced here: 460 us
  waiting for transfers between devices  335 us (73%)
  starting transfers between devices  77.7 us (17%)
  between operations  14.3 us (3%)
  matrix products  12.6 us (3%)
  local copies, waits for them, and re-layouts  12.2 us (3%)
  other arithmetic  8.02 us (2%)
    psum x1, waiting for transfers between devices, per_device(): lax.psum(jnp.einsum('tbk,kd->tbd', attention, out_proj, preferred_element...  244 us
    ppermute x15, starting transfers between devices, passed_along(): return lax.ppermute(block, axis, route)  77.6 us
    all_gather x1, waiting for transfers between devices, per_device(): row_piece = lax.all_gather(slot_rows, 'seq', axis=0, tiled=True)  59.7 us
    ppermute x15, waiting for transfers between devices, passed_along(): return lax.ppermute(block, axis, route)  31.7 us
  transfers between devices with their start and end apart: 17, of which 17 were waited for; matrix products, arithmetic and copies ran while one was open for 1% of the time, Pallas kernels for 0%

commit v1 on v0

v1 whole, which is shorter than its diff:
```python
import functools

import jax
import jax.numpy as jnp
from jax import lax
from jax.experimental import pallas as pl
from jax.experimental.pallas import tpu as pltpu
from jax.sharding import PartitionSpec as P

MESH = pl.DeviceIdType.MESH
BF = jnp.bfloat16
F32 = jnp.float32
SIDE = 4
CHIPS = 16
LC = 128
HS = 128
SLOTS = 32
ST = 2 * HS + 8


def dot(a, b, dims):
    return lax.dot_general(a, b, (dims, ((), ())), preferred_element_type=F32)


NN = ((1,), (0,))
NT = ((1,), (1,))
TN = ((0,), (0,))


def split(a):
    hi = a.astype(BF)
    return hi, (a - hi.astype(F32)).astype(BF)


def remote(src, dst, send, recv, peer):
    return pltpu.make_async_remote_copy(
        src, dst, send, recv, device_id=peer, device_id_type=MESH
    )


def kernel(
    q_ref,
    k_ref,
    v_ref,
    ld_ref,
    hg_ref,
    res_ref,
    outp_ref,
    ng_ref,
    rt_ref,
    wt_ref,
    wg_ref,
    wu_ref,
    attn_ref,
    hid_ref,
    ybuf,
    xbuf,
    prefix,
    inc,
    inner,
    grow,
    att,
    w2,
    part,
    own,
    rsbuf,
    resbuf,
    res16,
    mix,
    nrm,
    rts,
    wts,
    picks,
    slots,
    other,
    sw,
    wgb,
    wub,
    lsem,
    ysend,
    yrecv,
    xsend,
    xrecv,
    bsend,
    brecv,
    zsend,
    zrecv,
    gsend,
    grecv,
    ssend,
    srecv,
):
    s = lax.axis_index("seq")
    e = lax.axis_index("exp")
    x, y, z, c = s // SIDE, s % SIDE, e // 2, e % 2
    half = mix.shape[2]
    depth = 2 * half

    def at(xx, yy, zz, cc):
        return (xx * SIDE + yy, zz * 2 + cc)

    sib = at(x, y, z, 1 - c)
    barrier = pltpu.get_barrier_semaphore()

    def greet(peer):
        pl.semaphore_signal(barrier, inc=1, device_id=peer, device_id_type=MESH)

    greet(sib)
    for d in range(1, SIDE):
        greet(at(x, (y + d) % SIDE, z, c))
        greet(at((x + d) % SIDE, y, z, c))

    def greet_z(d, _):
        greet(at(x, y, (z + d) % CHIPS, c))
        return 0

    lax.fori_loop(1, CHIPS, greet_z, 0)

    mine = pl.ds(pl.multiple_of(c * half, half), half)
    theirs = pl.ds(pl.multiple_of((1 - c) * half, half), half)
    own_k = pl.ds(pl.multiple_of(c * HS, HS), HS)
    w2_own = pltpu.make_async_copy(outp_ref.at[:, mine], w2.at[own_k, :], lsem.at[0])
    wg_copy = pltpu.make_async_copy(wg_ref.at[0], wgb, lsem.at[1])
    wu_copy = pltpu.make_async_copy(wu_ref.at[0], wub, lsem.at[2])
    w2_own.start()
    wg_copy.start()
    wu_copy.start()

    ti = lax.broadcasted_iota(jnp.int32, (LC, LC), 0)
    ji = lax.broadcasted_iota(jnp.int32, (LC, LC), 1)
    causal = ji <= ti
    run_cols, run_rows = [], []
    for b in range(2):
        lb = jnp.broadcast_to(ld_ref[b], (LC, LC))
        rc = jnp.sum(jnp.where(causal, lb, 0.0), axis=1, keepdims=True)
        rr = jnp.sum(jnp.where(ji == ti, rc, 0.0), axis=0, keepdims=True)
        run_cols.append(rc)
        run_rows.append(rr)
        total = rr[:, LC - 1 :]
        kw = k_ref[b].astype(F32) * jnp.exp(total - rc)
        hi, lo = split(kw)
        vb = v_ref[b]
        ybuf[y, pl.ds(b * HS, HS), :] = dot(hi, vb, TN) + dot(lo, vb, TN)
        ybuf[y, pl.ds(2 * HS + b, 1), :] = jnp.broadcast_to(total, (1, HS))
    ybuf[y, pl.ds(2 * HS + 2, 6), :] = jnp.zeros((6, HS), F32)

    pl.semaphore_wait(barrier, 2 * (SIDE - 1) + CHIPS)

    ycopies = []
    for d in range(1, SIDE):
        cp = remote(
            ybuf.at[y], ybuf.at[y], ysend.at[d], yrecv.at[y], at(x, (y + d) % SIDE, z, c)
        )
        cp.start()
        ycopies.append(cp)
    w2_sib = remote(outp_ref.at[:, theirs], w2.at[own_k, :], bsend.at[0], brecv.at[0], sib)
    w2_sib.start()
    res_sib = remote(res_ref, resbuf.at[c], bsend.at[1], brecv.at[1], sib)
    res_sib.start()
    resbuf[c] = res_ref[...]

    for b in range(2):
        rc, rr = run_cols[b], run_rows[b]
        decay = jnp.where(causal, jnp.exp(jnp.where(causal, rc - rr, 0.0)), 0.0)
        hi, lo = split(dot(q_ref[b], k_ref[b], NT) * decay)
        vb = v_ref[b]
        inner[b] = dot(hi, vb, NN) + dot(lo, vb, NN)
        grow[b] = jnp.broadcast_to(jnp.exp(rc), (LC, HS))

    for d in range(1, SIDE):
        yy = (y + d) % SIDE
        remote(
            ybuf.at[yy], ybuf.at[yy], ysend.at[d], yrecv.at[yy], at(x, yy, z, c)
        ).wait_recv()
    for b in range(2):
        rows = pl.ds(b * HS, HS)
        run = jnp.zeros((HS, HS), F32)
        logs = jnp.zeros((1, HS), F32)
        pre = jnp.zeros((HS, HS), F32)
        prelog = jnp.zeros((1, HS), F32)
        for i in range(SIDE):
            pre = jnp.where(y == i, run, pre)
            prelog = jnp.where(y == i, logs, prelog)
            tot = ybuf[i, pl.ds(2 * HS + b, 1), :]
            run = jnp.exp(tot) * run + ybuf[i, rows, :]
            logs = logs + tot
        prefix[rows, :] = pre
        prefix[pl.ds(2 * HS + b, 1), :] = prelog
        xbuf[x, rows, :] = run
        xbuf[x, pl.ds(2 * HS + b, 1), :] = logs
    xbuf[x, pl.ds(2 * HS + 2, 6), :] = jnp.zeros((6, HS), F32)
    for d in range(1, SIDE):

        @pl.when(x + d < SIDE)
        def _():
            remote(
                xbuf.at[x], xbuf.at[x], xsend.at[d], xrecv.at[x], at((x + d) % SIDE, y, z, c)
            ).start()

    for b in range(2):
        for kk in range(2):
            for blk in range(CHIPS):
                cols = pl.ds(blk * LC, LC)
                rts[b * 2 + kk, pl.ds(blk, 1), :] = rt_ref[b, pl.ds(kk, 1), cols]
                wts[b * 2 + kk, pl.ds(blk, 1), :] = wt_ref[b, pl.ds(kk, 1), cols]
    before = (ti < ji).astype(F32).astype(BF)
    slot_id = lax.broadcasted_iota(jnp.int32, (SLOTS, LC), 0).astype(F32)
    ri = lax.broadcasted_iota(jnp.int32, (2 * LC, 2 * LC), 0)
    ci = lax.broadcasted_iota(jnp.int32, (2 * LC, 2 * LC), 1)
    rb, rtm = ri // LC, ri % LC
    perm = (ci == (rtm // 8) * 16 + rb * 8 + rtm % 8).astype(F32).astype(BF)

    def places(h0, h1):
        first = dot((h0 + h1).astype(BF), before, NN)
        return first, first + h0

    for ex in range(2):
        hits = []
        for b in range(2):
            r0 = rts[b * 2, pl.ds(s, 1), :]
            r1 = rts[b * 2 + 1, pl.ds(s, 1), :]
            hit = ((r0 == z * 2 + ex) | (r1 == z * 2 + ex)).astype(F32)
            hits.append(jnp.broadcast_to(hit, (8, LC)))
        p0, p1 = places(hits[0], hits[1])
        table = []
        for hh, pp in ((hits[0], p0), (hits[1], p1)):
            one = jnp.where(slot_id == pp[0:1, :], hh[0:1, :], 0.0)
            table.append(one)
        table = jnp.concatenate(table, axis=1).astype(BF)
        picks[pl.ds(ex * SLOTS, SLOTS), :] = dot(table, perm, NN).astype(BF)

    hits = [((rts[b * 2] == e) | (rts[b * 2 + 1] == e)).astype(F32) for b in range(2)]
    tws = [
        jnp.where(rts[b * 2] == e, wts[b * 2], 0.0)
        + jnp.where(rts[b * 2 + 1] == e, wts[b * 2 + 1], 0.0)
        for b in range(2)
    ]
    ranks = places(hits[0], hits[1])
    for blk in range(CHIPS):
        acc = jnp.zeros((8, SLOTS), F32)
        for b in range(2):
            row = slice(blk, blk + 1)
            one = jnp.where(slot_id == ranks[b][row], hits[b][row], 0.0).astype(BF)
            w = jnp.broadcast_to(tws[b][row], (8, LC))
            hi = w.astype(BF)
            rest = w - hi.astype(F32)
            mid, low = split(rest)
            acc = acc + (dot(hi, one, NT) + (dot(mid, one, NT) + dot(low, one, NT)))
        sw[:, pl.ds(blk * SLOTS, SLOTS)] = acc

    inc[...] = jnp.zeros_like(inc)
    for i in range(SIDE - 1):

        @pl.when(x > i)
        def _():
            remote(
                xbuf.at[i], xbuf.at[i], xsend.at[0], xrecv.at[i], at(i, y, z, c)
            ).wait_recv()
            for b in range(2):
                rows = pl.ds(b * HS, HS)
                tot = xbuf[i, pl.ds(2 * HS + b, 1), :]
                inc[rows, :] = jnp.exp(tot) * inc[rows, :] + xbuf[i, rows, :]

    heads = []
    for b in range(2):
        rows = pl.ds(b * HS, HS)
        state = prefix[rows, :] + jnp.exp(prefix[pl.ds(2 * HS + b, 1), :]) * inc[rows, :]
        hi, lo = split(state)
        qb = q_ref[b]
        raw = inner[b] + grow[b] * (dot(qb, hi, NN) + dot(qb, lo, NN))
        meansq = jnp.mean(raw * raw, axis=1, keepdims=True)
        heads.append((raw * lax.rsqrt(meansq + 1e-06) * hg_ref[...]).reshape(CHIPS, 1, 8, HS))
    att[:, own_k] = jnp.concatenate(heads, axis=1).reshape(2 * LC, HS).astype(BF)
    att_sib = remote(att.at[:, own_k], att.at[:, own_k], bsend.at[2], brecv.at[2], sib)
    att_sib.start()

    w2_own.wait()
    other_k = pl.ds(pl.multiple_of((1 - c) * HS, HS), HS)
    remote(outp_ref.at[:, theirs], w2.at[other_k, :], bsend.at[0], brecv.at[0], sib).wait_recv()
    remote(att.at[:, own_k], att.at[:, other_k], bsend.at[2], brecv.at[2], sib).wait_recv()
    own_rows = pl.ds(pl.multiple_of(z * 16, 16), 16)
    for j in range(half // 256):
        cols = pl.ds(j * 256, 256)
        part[:, cols] = dot(att[...], w2[:, cols], NN).astype(BF)
    own[...] = dot(att[own_rows, :], w2[...], NN)

    def far_first(i):
        return CHIPS // 2 + ((i + 1) // 2) * (1 - 2 * (i % 2))

    def send_part(i, _):
        zz = (z + far_first(i)) % CHIPS
        rows = pl.ds(pl.multiple_of(zz * 16, 16), 16)
        remote(
            part.at[rows, :], rsbuf.at[own_rows, :], zsend.at[zz], zrecv.at[z], at(x, y, zz, c)
        ).start()
        return 0

    lax.fori_loop(0, CHIPS - 1, send_part, 0)

    remote(res_ref, resbuf.at[1 - c], bsend.at[1], brecv.at[1], sib).wait_recv()
    for cc in range(2):
        for i in range(4):
            two = resbuf[cc, i, :, mine].astype(F32)
            for b in range(2):
                res16[pl.ds(b * 8 + cc * 4 + i, 1), :] = two[b : b + 1, :]

    def wait_part(d, _):
        zz = (z + d) % CHIPS
        rows = pl.ds(pl.multiple_of(zz * 16, 16), 16)
        remote(
            part.at[rows, :], rsbuf.at[rows, :], zsend.at[zz], zrecv.at[zz], at(x, y, zz, c)
        ).wait_recv()
        return 0

    lax.fori_loop(1, CHIPS, wait_part, 0)
    acc = own[...] + res16[...]
    for d in range(1, CHIPS):
        rows = pl.ds(pl.multiple_of(((z + d) % CHIPS) * 16, 16), 16)
        acc = acc + rsbuf[rows, :].astype(F32)
    mix[c] = acc
    mix_sib = remote(mix.at[c], mix.at[c], bsend.at[3], brecv.at[3], sib)
    mix_sib.start()
    ss = jnp.sum(acc * acc, axis=1, keepdims=True)
    remote(mix.at[c], mix.at[1 - c], bsend.at[3], brecv.at[3], sib).wait_recv()
    far = mix[1 - c]
    ss = ss + jnp.sum(far * far, axis=1, keepdims=True)
    scale = lax.rsqrt(ss * (1.0 / depth) + 1e-06)
    nrm[own_rows, :] = (mix[c] * scale * ng_ref[:, mine]).astype(BF)

    def send_norm(i, _):
        zz = (z + far_first(i)) % CHIPS
        remote(
            nrm.at[own_rows, :], nrm.at[own_rows, :], gsend.at[zz], grecv.at[z], at(x, y, zz, c)
        ).start()
        return 0

    lax.fori_loop(0, CHIPS - 1, send_norm, 0)
    for h in range(2):
        for b in range(2):
            for i in range(4):
                attn_ref[i, pl.ds(b, 1), pl.ds(h * half, half)] = mix[
                    h, pl.ds(b * 8 + c * 4 + i, 1), :
                ]

    def wait_norm(d, _):
        zz = (z + d) % CHIPS
        rows = pl.ds(pl.multiple_of(zz * 16, 16), 16)
        remote(
            nrm.at[rows, :], nrm.at[rows, :], gsend.at[zz], grecv.at[zz], at(x, y, zz, c)
        ).wait_recv()
        return 0

    lax.fori_loop(1, CHIPS, wait_norm, 0)

    blk_rows = pl.ds(pl.multiple_of(s * SLOTS, SLOTS), SLOTS)
    theirs_p = pl.ds(pl.multiple_of((1 - c) * SLOTS, SLOTS), SLOTS)
    mine_p = pl.ds(pl.multiple_of(c * SLOTS, SLOTS), SLOTS)
    other[...] = dot(picks[theirs_p, :], nrm[...], NN).astype(BF)
    pick_sib = remote(other, slots.at[c, blk_rows, :], bsend.at[4], brecv.at[4], sib)
    pick_sib.start()
    slots[c, blk_rows, :] = dot(picks[mine_p, :], nrm[...], NN).astype(BF)
    remote(other, slots.at[1 - c, blk_rows, :], bsend.at[4], brecv.at[4], sib).wait_recv()

    def piece(h, bx, by, sem, peer):
        blk = bx * SIDE + by
        rows = pl.ds(pl.multiple_of(blk * SLOTS, SLOTS), SLOTS)
        ref = slots.at[h, rows, :]
        return remote(ref, ref, ssend.at[h, sem], srecv.at[h, blk], peer)

    for d in range(1, SIDE):
        piece(0, x, y, d, at((x + d) % SIDE, y, z, c)).start()
        piece(1, x, y, d, at(x, (y + d) % SIDE, z, c)).start()
    for m in range(SIDE):
        xx, yy = (x + m) % SIDE, (y + m) % SIDE
        if m:
            piece(0, xx, y, 0, sib).wait_recv()
        for d in range(1, SIDE):
            piece(0, xx, y, SIDE * (m + 1) + d, at(x, (y + d) % SIDE, z, c)).start()
        if m:
            piece(1, x, yy, 0, sib).wait_recv()
        for d in range(1, SIDE):
            piece(1, x, yy, SIDE * (m + 1) + d, at((x + d) % SIDE, y, z, c)).start()
    for m in range(SIDE):
        xx, yy = (x + m) % SIDE, (y + m) % SIDE
        for d in range(1, SIDE):
            piece(0, xx, (y + d) % SIDE, 0, sib).wait_recv()
            piece(1, (x + d) % SIDE, yy, 0, sib).wait_recv()

    wg_copy.wait()
    wu_copy.wait()
    for n in range(2):
        rows = pl.ds(n * 256, 256)
        gate = dot(wgb[:, :half], slots[0, rows, :], NT) + dot(wgb[:, half:], slots[1, rows, :], NT)
        up = dot(wub[:, :half], slots[0, rows, :], NT) + dot(wub[:, half:], slots[1, rows, :], NT)
        hid_ref[0, :, rows] = sw[0:1, rows] * (gate / (1.0 + jnp.exp(-gate))) * up

    for cp in ycopies:
        cp.wait_send()
    for d in range(1, SIDE):

        @pl.when(x + d < SIDE)
        def _():
            remote(
                xbuf.at[x], xbuf.at[x], xsend.at[d], xrecv.at[x], at((x + d) % SIDE, y, z, c)
            ).wait_send()

    for cp in (w2_sib, res_sib, att_sib, mix_sib, pick_sib):
        cp.wait_send()

    def drain(d, _):
        zz = (z + d) % CHIPS
        rows = pl.ds(pl.multiple_of(zz * 16, 16), 16)
        peer = at(x, y, zz, c)
        remote(part.at[rows, :], rsbuf.at[own_rows, :], zsend.at[zz], zrecv.at[z], peer).wait_send()
        remote(
            nrm.at[own_rows, :], nrm.at[own_rows, :], gsend.at[zz], grecv.at[z], peer
        ).wait_send()
        return 0

    lax.fori_loop(1, CHIPS, drain, 0)
    for h in range(2):
        for m in range(SIDE + 1):
            for d in range(1, SIDE):
                piece(h, x, y, SIDE * m + d, sib).wait_send()


def per_device(
    residual,
    queries,
    key_vecs,
    value_vecs,
    log_decay,
    head_gain,
    out_proj,
    norm_gain,
    routes,
    route_weight,
    w_gate,
    w_up,
):
    model_width = residual.shape[2]
    half = model_width // 2
    hidden = w_gate.shape[1]
    vmem = pl.BlockSpec(memory_space=pltpu.VMEM)
    hbm = pl.BlockSpec(memory_space=pl.ANY)
    dma = pltpu.SemaphoreType.DMA
    spans = CHIPS * SLOTS
    return pl.pallas_call(
        kernel,
        out_shape=(
            jax.ShapeDtypeStruct(residual.shape, F32),
            jax.ShapeDtypeStruct((1, hidden, spans), F32),
        ),
        in_specs=[vmem] * 6 + [hbm] + [vmem] * 3 + [hbm] * 2,
        out_specs=(vmem, vmem),
        scratch_shapes=[
            pltpu.VMEM((SIDE, ST, HS), F32),
            pltpu.VMEM((SIDE, ST, HS), F32),
            pltpu.VMEM((ST, HS), F32),
            pltpu.VMEM((2 * HS, HS), F32),
            pltpu.VMEM((2, LC, HS), F32),
            pltpu.VMEM((2, LC, HS), F32),
            pltpu.VMEM((2 * LC, 2 * HS), BF),
            pltpu.VMEM((2 * HS, half), BF),
            pltpu.VMEM((2 * LC, half), BF),
            pltpu.VMEM((16, half), F32),
            pltpu.VMEM((2 * LC, half), BF),
            pltpu.VMEM((2,) + residual.shape, BF),
            pltpu.VMEM((16, half), F32),
            pltpu.VMEM((2, 16, half), F32),
            pltpu.VMEM((2 * LC, half), BF),
            pltpu.VMEM((4, CHIPS, LC), jnp.int32),
            pltpu.VMEM((4, CHIPS, LC), F32),
            pltpu.VMEM((2 * SLOTS, 2 * LC), BF),
            pltpu.VMEM((2, spans, half), BF),
            pltpu.VMEM((SLOTS, half), BF),
            pltpu.VMEM((8, spans), F32),
            pltpu.VMEM((hidden, model_width), BF),
            pltpu.VMEM((hidden, model_width), BF),
            dma((3,)),
            dma((SIDE,)),
            dma((SIDE,)),
            dma((SIDE,)),
            dma((SIDE,)),
            dma((5,)),
            dma((5,)),
            dma((CHIPS,)),
            dma((CHIPS,)),
            dma((CHIPS,)),
            dma((CHIPS,)),
            dma((2, SIDE * (SIDE + 1) + SIDE)),
            dma((2, CHIPS)),
        ],
        compiler_params=pltpu.CompilerParams(
            collective_id=0, has_side_effects=True, vmem_limit_bytes=48 << 20
        ),
        name="layer",
    )(
        queries,
        key_vecs,
        value_vecs,
        log_decay,
        head_gain.reshape(1, -1),
        residual,
        out_proj,
        norm_gain.reshape(1, -1),
        jnp.transpose(routes, (1, 2, 0)),
        jnp.transpose(route_weight, (1, 2, 0)),
        w_gate,
        w_up,
    )


def solution(mesh):
    placed = (
        P(("seq", "exp"), None, None),
        P(None, "seq", "exp"),
        P(None, "seq", "exp"),
        P(None, "seq", "exp"),
        P(None, "exp", "seq"),
        P("exp"),
        P("exp", None),
        P(),
        P(),
        P(),
        P("exp", "seq", None),
        P("exp", "seq", None),
    )
    return jax.shard_map(
        per_device,
        mesh=mesh,
        in_specs=placed,
        out_specs=(P(("seq", "exp"), None, None), P("exp", "seq", None)),
        check_vma=False,
    )
```

time: 461 us -> 150 us (0.33)
  waiting for transfers between devices: 335 us -> 0 us
  Pallas kernels: 0 us -> 136 us
  starting transfers between devices: 77.7 us -> 0 us
  between operations: 14.3 us -> 0.66 us
  matrix products: 12.6 us -> 0 us
  other arithmetic: 8.02 us -> 0 us
    psum x1 -> x0, waiting for transfers between devices: 244 us -> none  [per_device(): lax.psum(jnp.einsum('tbk,kd->tbd', attention, out_proj, preferred_element...]
    pallas_call x0 -> x1, Pallas kernels: none -> 136 us  [per_device(): pl.pallas_call(kernel, out_shape=(jax.ShapeDtypeStruct(residual.shape, F3...]
    ppermute x15 -> x0, starting transfers between devices: 77.6 us -> none  [passed_along(): return lax.ppermute(block, axis, route)]
    all_gather x1 -> x0, waiting for transfers between devices: 59.7 us -> none  [per_device(): row_piece = lax.all_gather(slot_rows, 'seq', axis=0, tiled=True)]
    ppermute x15 -> x0, waiting for transfers between devices: 31.7 us -> none  [passed_along(): return lax.ppermute(block, axis, route)]
    dot_general x9 -> x0, matrix products: 12.6 us -> none  [the longest x1 3.15 us: per_device(): lax.dot_general(w_gate[0], row_piece, (((1,), (1,)), ((), ())), preferred...]
    unnamed x23 -> x26, local copies, waits for them, and re-layouts: 1.26 us -> 12.4 us
  transfers between devices with their start and end apart: 17 -> 0, of which waited for: 17 -> 0; matrix products, arithmetic and copies ran while one was open for 1% -> 0% of each run, Pallas kernels for 0% -> 0%
where the time goes in v1:
time: 150 us; the launch traced here: 149 us
  Pallas kernels  136 us (91%)
  local copies, waits for them, and re-layouts  12.4 us (8%)
    pallas_call x1, Pallas kernels, per_device(): pl.pallas_call(kernel, out_shape=(jax.ShapeDtypeStruct(residual.shape, F3...  136 us
    unnamed x26, local copies, waits for them, and re-layouts  12.4 us

profile of v1, /device:TPU:1, one launch (start us, length us, event | category | flops | bytes accessed | tf_op | source)
XLA Modules:
  0.0 149.5 jit_solution(841202056952624368)
XLA Ops:
  0.6 0.0 copy-start
  0.6 1.5 copy-done
  2.1 0.0 copy-start.1
  2.1 1.5 copy-done.1
  3.6 0.0 copy-start.2
  3.6 1.1 copy-done.2
  4.7 0.0 copy-start.3
  4.7 0.8 copy-done.3
  5.6 0.0 copy-start.4
  5.6 0.8 copy-done.4
  6.4 0.0 copy-start.5
  6.4 0.8 copy-done.5
  7.2 0.0 copy-start.6
  7.2 0.8 copy-done.6
  8.0 0.0 copy-start.7
  8.0 0.8 copy-done.7
  8.8 0.0 copy-start.8
  8.8 0.8 copy-done.8
  9.6 0.0 copy-start.9
  9.6 0.7 copy-done.9
  10.3 0.0 copy-start.10
  10.3 0.7 copy-done.10
  10.9 0.0 copy-start.11
  10.9 0.7 copy-done.11
  11.6 136.4 %layer.1 = (f32[4,2,3072]{2,1,0:T(2,128)S(1)}, f32[1,288,512]{2,1,0:T(8,128)S(1)}) custom-call(bf16[2,128,128]{2,1,0:T(8,128)(2,1)S(1)} %copy-done.3, bf16[2,128,128]{2,1,0:T(8,128)(2,1)S(1)} %copy-done.4, bf16[2,128,128]{2,1,0:T(8,128)(2,1)S(1)} %copy-done.5, f32[2,1,128]{2,1,0:T(1,128)S(1)} %copy-done.10, f32[1,128]{1,0:T(1,128)S(1)} %bitcast.7, ...), custom_call_target="tpu_custom_call" | custom-call | tf_op jit(solution)/shard_map/layer/pallas_call | solution.py:448
  148.0 0.6 copy.16
  148.7 0.8 copy.17
Async XLA Ops:
  0.6 1.5 copy-start
  2.1 1.5 copy-start.1
  3.6 1.1 copy-start.2
  4.7 0.8 copy-start.3
  5.6 0.8 copy-start.4
  6.4 0.8 copy-start.5
  7.2 0.8 copy-start.6
  8.0 0.8 copy-start.7
  8.8 0.8 copy-start.8
  9.6 0.7 copy-start.9
  10.3 0.7 copy-start.10
  10.9 0.7 copy-start.11

commit v2 on v1

--- a/solution.py
+++ b/solution.py
@@ -15,6 +15,17 @@
 LC = 128
 HS = 128
 SLOTS = 32
+PARTS = 3
+EXTRA = 128
+PARENT = {
+    1: 0, 3: 0, 6: 0, 2: 3, 4: 3, 5: 6, 7: 6, 8: 6,
+    -1: 0, -3: 0, -6: 0, -2: -3, -4: -3, -5: -6, -7: -6,
+}
+OFFS = list(PARENT)
+CHILDREN = {p: [o for o in OFFS if PARENT[o] == p] for p in (0, 3, 6, -3, -6)}
+LEAVES = [o for o in OFFS if o not in CHILDREN]
+RELAYS = [o for o in OFFS if o in CHILDREN]
+REACH = sorted({PARENT[o] - o for o in OFFS} | {o - PARENT[o] for o in OFFS})
 ST = 2 * HS + 8
 
 
@@ -39,20 +50,28 @@
 
 
 def kernel(
+    q_hbm,
+    k_hbm,
+    v_hbm,
+    ld_hbm,
+    hg_hbm,
+    res_hbm,
+    outp_ref,
+    ng_hbm,
+    rt_hbm,
+    wt_hbm,
+    wg_ref,
+    wu_ref,
+    attn_ref,
+    hid_ref,
     q_ref,
     k_ref,
     v_ref,
     ld_ref,
     hg_ref,
-    res_ref,
-    outp_ref,
     ng_ref,
     rt_ref,
     wt_ref,
-    wg_ref,
-    wu_ref,
-    attn_ref,
-    hid_ref,
     ybuf,
     xbuf,
     prefix,
@@ -62,8 +81,9 @@
     att,
     w2,
     part,
-    own,
+    full,
     rsbuf,
+    rly,
     resbuf,
     res16,
     mix,
@@ -76,6 +96,8 @@
     sw,
     wgb,
     wub,
+    gacc,
+    uacc,
     lsem,
     ysend,
     yrecv,
@@ -87,6 +109,8 @@
     zrecv,
     gsend,
     grecv,
+    psend,
+    precv,
     ssend,
     srecv,
 ):
@@ -96,6 +120,12 @@
     half = mix.shape[2]
     depth = 2 * half
 
+    drains = []
+
+    def finish():
+        for wait in drains:
+            wait()
+
     def at(xx, yy, zz, cc):
         return (xx * SIDE + yy, zz * 2 + cc)
 
@@ -110,11 +140,8 @@
         greet(at(x, (y + d) % SIDE, z, c))
         greet(at((x + d) % SIDE, y, z, c))
 
-    def greet_z(d, _):
+    for d in REACH:
         greet(at(x, y, (z + d) % CHIPS, c))
-        return 0
-
-    lax.fori_loop(1, CHIPS, greet_z, 0)
 
     mine = pl.ds(pl.multiple_of(c * half, half), half)
     theirs = pl.ds(pl.multiple_of((1 - c) * half, half), half)
@@ -122,9 +149,29 @@
     w2_own = pltpu.make_async_copy(outp_ref.at[:, mine], w2.at[own_k, :], lsem.at[0])
     wg_copy = pltpu.make_async_copy(wg_ref.at[0], wgb, lsem.at[1])
     wu_copy = pltpu.make_async_copy(wu_ref.at[0], wub, lsem.at[2])
+    ins = [
+        pltpu.make_async_copy(a, b, lsem.at[3 + i])
+        for i, (a, b) in enumerate(
+            (
+                (ld_hbm, ld_ref),
+                (k_hbm, k_ref),
+                (v_hbm, v_ref),
+                (q_hbm, q_ref),
+                (rt_hbm, rt_ref),
+                (wt_hbm, wt_ref),
+                (hg_hbm, hg_ref),
+                (ng_hbm, ng_ref),
+                (res_hbm, resbuf.at[c]),
+            )
+        )
+    ]
+    for cp in ins:
+        cp.start()
     w2_own.start()
     wg_copy.start()
     wu_copy.start()
+    for cp in ins[:3]:
+        cp.wait()
 
     ti = lax.broadcasted_iota(jnp.int32, (LC, LC), 0)
     ji = lax.broadcasted_iota(jnp.int32, (LC, LC), 1)
@@ -144,20 +191,22 @@
         ybuf[y, pl.ds(2 * HS + b, 1), :] = jnp.broadcast_to(total, (1, HS))
     ybuf[y, pl.ds(2 * HS + 2, 6), :] = jnp.zeros((6, HS), F32)
 
-    pl.semaphore_wait(barrier, 2 * (SIDE - 1) + CHIPS)
-
-    ycopies = []
+    pl.semaphore_wait(barrier, 2 * (SIDE - 1) + 1 + len(REACH))
+
     for d in range(1, SIDE):
         cp = remote(
             ybuf.at[y], ybuf.at[y], ysend.at[d], yrecv.at[y], at(x, (y + d) % SIDE, z, c)
         )
         cp.start()
-        ycopies.append(cp)
+        drains.append(cp.wait_send)
     w2_sib = remote(outp_ref.at[:, theirs], w2.at[own_k, :], bsend.at[0], brecv.at[0], sib)
     w2_sib.start()
-    res_sib = remote(res_ref, resbuf.at[c], bsend.at[1], brecv.at[1], sib)
+    drains.append(w2_sib.wait_send)
+    res_sib = remote(res_hbm, resbuf.at[c], bsend.at[1], brecv.at[1], sib)
     res_sib.start()
-    resbuf[c] = res_ref[...]
+    drains.append(res_sib.wait_send)
+    for cp in ins[3:]:
+        cp.wait()
 
     for b in range(2):
         rc, rr = run_cols[b], run_rows[b]
@@ -197,6 +246,17 @@
                 xbuf.at[x], xbuf.at[x], xsend.at[d], xrecv.at[x], at((x + d) % SIDE, y, z, c)
             ).start()
 
+    def drain_x():
+        for d in range(1, SIDE):
+
+            @pl.when(x + d < SIDE)
+            def _():
+                remote(
+                    xbuf.at[x], xbuf.at[x], xsend.at[d], xrecv.at[x], at((x + d) % SIDE, y, z, c)
+                ).wait_send()
+
+    drains.append(drain_x)
+
     for b in range(2):
         for kk in range(2):
             for blk in range(CHIPS):
@@ -273,155 +333,218 @@
     att[:, own_k] = jnp.concatenate(heads, axis=1).reshape(2 * LC, HS).astype(BF)
     att_sib = remote(att.at[:, own_k], att.at[:, own_k], bsend.at[2], brecv.at[2], sib)
     att_sib.start()
+    drains.append(att_sib.wait_send)
 
     w2_own.wait()
     other_k = pl.ds(pl.multiple_of((1 - c) * HS, HS), HS)
     remote(outp_ref.at[:, theirs], w2.at[other_k, :], bsend.at[0], brecv.at[0], sib).wait_recv()
     remote(att.at[:, own_k], att.at[:, other_k], bsend.at[2], brecv.at[2], sib).wait_recv()
-    own_rows = pl.ds(pl.multiple_of(z * 16, 16), 16)
-    for j in range(half // 256):
-        cols = pl.ds(j * 256, 256)
-        part[:, cols] = dot(att[...], w2[:, cols], NN).astype(BF)
-    own[...] = dot(att[own_rows, :], w2[...], NN)
-
-    def far_first(i):
-        return CHIPS // 2 + ((i + 1) // 2) * (1 - 2 * (i % 2))
-
-    def send_part(i, _):
-        zz = (z + far_first(i)) % CHIPS
-        rows = pl.ds(pl.multiple_of(zz * 16, 16), 16)
+    width = half // PARTS
+
+    def rows_of(zz):
+        return pl.ds(pl.multiple_of((zz % CHIPS) * 16, 16), 16)
+
+    def span(p):
+        return pl.ds(p * width, width + (EXTRA if p == PARTS - 1 else 0))
+
+    def send(cp):
+        cp.start()
+        drains.append(cp.wait_send)
+
+    own_rows = rows_of(z)
+
+    def rs_copy(o, p, src):
+        i = OFFS.index(o)
+        peer = at(x, y, (z - o + PARENT[o]) % CHIPS, c)
+        dst = rsbuf.at[i, :, pl.ds(p * width, width)]
+        return remote(src, dst, zsend.at[i, p], zrecv.at[i, p], peer)
+
+    def rs_arrived(o, p):
+        cols = pl.ds(p * width, width)
+        i = OFFS.index(o)
+        ref = rsbuf.at[i, :, cols]
+        remote(ref, ref, zsend.at[i, p], zrecv.at[i, p], sib).wait_recv()
+        return rsbuf[i, :, cols].astype(F32)
+
+    def project(p):
+        cols = pl.ds(p * width, width)
+        got = dot(att[...], w2[:, cols], NN)
+        full[:, cols] = got
+        part[:, cols] = got.astype(BF)
+        for o in LEAVES:
+            send(rs_copy(o, p, part.at[rows_of(z - o), cols]))
+
+    def relay(p):
+        cols = pl.ds(p * width, width)
+        for o in RELAYS:
+            acc = full[rows_of(z - o), cols]
+            for ch in CHILDREN[o]:
+                acc = acc + rs_arrived(ch, p)
+            r = RELAYS.index(o)
+            rly[r, :, cols] = acc.astype(BF)
+            send(rs_copy(o, p, rly.at[r, :, cols]))
+
+    def ag_copy(o, p, src_z, peer):
+        i = OFFS.index(o)
+        ref = nrm.at[rows_of(src_z), span(p)]
+        return remote(ref, ref, gsend.at[i, p], grecv.at[i, p], peer)
+
+    def total(p):
+        cols = pl.ds(p * width, width)
+        acc = full[own_rows, cols] + res16[:, cols]
+        for ch in CHILDREN[0]:
+            acc = acc + rs_arrived(ch, p)
+        mix[c, :, cols] = acc
+        gain = ng_ref[:, pl.ds(pl.multiple_of(c * half + p * width, 128), width)]
+        nrm[own_rows, cols] = (acc * gain).astype(BF)
+        if p == PARTS - 1:
+            mix_sib = remote(mix.at[c], mix.at[c], bsend.at[3], brecv.at[3], sib)
+            send(mix_sib)
+            near = mix[c]
+            ss = jnp.sum(near * near, axis=1, keepdims=True)
+            remote(mix.at[c], mix.at[1 - c], bsend.at[3], brecv.at[3], sib).wait_recv()
+            far = mix[1 - c]
+            ss = ss + jnp.sum(far * far, axis=1, keepdims=True)
+            scale = lax.rsqrt(ss * (1.0 / depth) + 1e-06)
+            hi = scale.astype(BF).astype(F32)
+            mid = (scale - hi).astype(BF).astype(F32)
+            low = scale - hi - mid
+            lane = lax.broadcasted_iota(jnp.int32, (16, EXTRA), 1)
+            extra = jnp.where(
+                lane == 0, hi, jnp.where(lane == 1, mid, jnp.where(lane == 2, low, 0.0))
+            )
+            nrm[own_rows, pl.ds(half, EXTRA)] = extra.astype(BF)
+        for o in CHILDREN[0]:
+            send(ag_copy(o, p, z, at(x, y, (z + o) % CHIPS, c)))
+
+    def forward(p):
+        for o in RELAYS:
+            ag_copy(o, p, z - o, sib).wait_recv()
+            for ch in CHILDREN[o]:
+                send(ag_copy(ch, p, z - o, at(x, y, (z - o + ch) % CHIPS, c)))
+
+    theirs_p = pl.ds(pl.multiple_of((1 - c) * SLOTS, SLOTS), SLOTS)
+    mine_p = pl.ds(pl.multiple_of(c * SLOTS, SLOTS), SLOTS)
+
+    def pick(p):
+        for o in LEAVES:
+            ag_copy(o, p, z - o, sib).wait_recv()
+        cols = span(p)
+        other[:, cols] = dot(picks[theirs_p, :], nrm[:, cols], NN).astype(BF)
+        send(
+            remote(
+                other.at[:, cols], slots.at[c, x, y, :, cols], psend.at[p], precv.at[p], sib
+            )
+        )
+        slots[c, x, y, :, cols] = dot(picks[mine_p, :], nrm[:, cols], NN).astype(BF)
+
+    def parts_of(p):
+        size = width + (EXTRA if p == PARTS - 1 else 0)
+        left = size // 256 * 128
+        return pl.ds(p * width, left), pl.ds(p * width + left, size - left)
+
+    def step1(h, d):
+        dx, dy = (d, 0) if h == 0 else (0, d)
+        return (x + dx) % SIDE, (y + dy) % SIDE
+
+    def step2(h, d):
+        dx, dy = (0, d) if h == 0 else (d, 0)
+        return (x + dx) % SIDE, (y + dy) % SIDE
+
+    def one(h, where, cols):
+        return slots.at[h, where[0], where[1], :, cols]
+
+    def four(h, where, cols):
+        if h == 0:
+            return slots.at[h, :, where[1], :, cols]
+        return slots.at[h, where[0], :, :, cols]
+
+    def xy(h, p, stage, i, ref, where):
+        return remote(
+            ref, ref, ssend.at[h, p, stage, i], srecv.at[h, p, stage, i], at(*where, z, c)
+        )
+
+    def hop1(p):
+        cols = span(p)
         remote(
-            part.at[rows, :], rsbuf.at[own_rows, :], zsend.at[zz], zrecv.at[z], at(x, y, zz, c)
-        ).start()
-        return 0
-
-    lax.fori_loop(0, CHIPS - 1, send_part, 0)
-
-    remote(res_ref, resbuf.at[1 - c], bsend.at[1], brecv.at[1], sib).wait_recv()
+            other.at[:, cols], slots.at[1 - c, x, y, :, cols], psend.at[p], precv.at[p], sib
+        ).wait_recv()
+        for h in range(2):
+            for i, d in enumerate((1, -1)):
+                send(xy(h, p, 0, i, one(h, (x, y), cols), step1(h, d)))
+
+    def hop2(p):
+        for h in range(2):
+            for i, d in enumerate((1, -1)):
+                back = step1(h, -d)
+                xy(h, p, 0, i, one(h, back, span(p)), back).wait_recv()
+                send(xy(h, p, 1, i, one(h, back, parts_of(p)[i]), step1(h, d)))
+
+    def hop3(p):
+        for h in range(2):
+            for i, d in enumerate((1, -1)):
+                far = step1(h, 2)
+                xy(h, p, 1, i, one(h, far, parts_of(p)[i]), far).wait_recv()
+            for i, d in enumerate((1, -1)):
+                send(xy(h, p, 2, i, four(h, (x, y), span(p)), step2(h, d)))
+
+    def hop4(p):
+        for h in range(2):
+            for i, d in enumerate((1, -1)):
+                back = step2(h, -d)
+                xy(h, p, 2, i, four(h, back, span(p)), back).wait_recv()
+                send(xy(h, p, 3, i, four(h, back, parts_of(p)[i]), step2(h, d)))
+
+    def multiply(p):
+        for h in range(2):
+            for i in range(2):
+                far = step2(h, 2)
+                xy(h, p, 3, i, four(h, far, parts_of(p)[i]), far).wait_recv()
+        if p == 0:
+            wg_copy.wait()
+            wu_copy.wait()
+        for n in range(2):
+            rows = pl.ds(n * 256, 256)
+            for w, acc in ((wgb, gacc), (wub, uacc)):
+                got = None
+                for h in range(2):
+                    rhs = slots[h, pl.ds(2 * n, 2), :, :, pl.ds(p * width, width)]
+                    rhs = rhs.reshape(256, width)
+                    term = dot(w[:, pl.ds(h * half + p * width, width)], rhs, NT)
+                    got = term if got is None else got + term
+                acc[:, rows] = got if p == 0 else acc[:, rows] + got
+
+    remote(res_hbm, resbuf.at[1 - c], bsend.at[1], brecv.at[1], sib).wait_recv()
     for cc in range(2):
         for i in range(4):
             two = resbuf[cc, i, :, mine].astype(F32)
             for b in range(2):
                 res16[pl.ds(b * 8 + cc * 4 + i, 1), :] = two[b : b + 1, :]
-
-    def wait_part(d, _):
-        zz = (z + d) % CHIPS
-        rows = pl.ds(pl.multiple_of(zz * 16, 16), 16)
-        remote(
-            part.at[rows, :], rsbuf.at[rows, :], zsend.at[zz], zrecv.at[zz], at(x, y, zz, c)
-        ).wait_recv()
-        return 0
-
-    lax.fori_loop(1, CHIPS, wait_part, 0)
-    acc = own[...] + res16[...]
-    for d in range(1, CHIPS):
-        rows = pl.ds(pl.multiple_of(((z + d) % CHIPS) * 16, 16), 16)
-        acc = acc + rsbuf[rows, :].astype(F32)
-    mix[c] = acc
-    mix_sib = remote(mix.at[c], mix.at[c], bsend.at[3], brecv.at[3], sib)
-    mix_sib.start()
-    ss = jnp.sum(acc * acc, axis=1, keepdims=True)
-    remote(mix.at[c], mix.at[1 - c], bsend.at[3], brecv.at[3], sib).wait_recv()
-    far = mix[1 - c]
-    ss = ss + jnp.sum(far * far, axis=1, keepdims=True)
-    scale = lax.rsqrt(ss * (1.0 / depth) + 1e-06)
-    nrm[own_rows, :] = (mix[c] * scale * ng_ref[:, mine]).astype(BF)
-
-    def send_norm(i, _):
-        zz = (z + far_first(i)) % CHIPS
-        remote(
-            nrm.at[own_rows, :], nrm.at[own_rows, :], gsend.at[zz], grecv.at[z], at(x, y, zz, c)
-        ).start()
-        return 0
-
-    lax.fori_loop(0, CHIPS - 1, send_norm, 0)
+    for p in range(PARTS):
+        project(p)
+    stages = [relay, total, forward, pick, hop1, hop2, hop3, hop4, multiply]
+    for t in range(len(stages) + PARTS - 1):
+        for p in range(PARTS):
+            if 0 <= t - p < len(stages):
+                stages[t - p](p)
+
     for h in range(2):
         for b in range(2):
             for i in range(4):
                 attn_ref[i, pl.ds(b, 1), pl.ds(h * half, half)] = mix[
                     h, pl.ds(b * 8 + c * 4 + i, 1), :
                 ]
-
-    def wait_norm(d, _):
-        zz = (z + d) % CHIPS
-        rows = pl.ds(pl.multiple_of(zz * 16, 16), 16)
-        remote(
-            nrm.at[rows, :], nrm.at[rows, :], gsend.at[zz], grecv.at[zz], at(x, y, zz, c)
-        ).wait_recv()
-        return 0
-
-    lax.fori_loop(1, CHIPS, wait_norm, 0)
-
-    blk_rows = pl.ds(pl.multiple_of(s * SLOTS, SLOTS), SLOTS)
-    theirs_p = pl.ds(pl.multiple_of((1 - c) * SLOTS, SLOTS), SLOTS)
-    mine_p = pl.ds(pl.multiple_of(c * SLOTS, SLOTS), SLOTS)
-    other[...] = dot(picks[theirs_p, :], nrm[...], NN).astype(BF)
-    pick_sib = remote(other, slots.at[c, blk_rows, :], bsend.at[4], brecv.at[4], sib)
-    pick_sib.start()
-    slots[c, blk_rows, :] = dot(picks[mine_p, :], nrm[...], NN).astype(BF)
-    remote(other, slots.at[1 - c, blk_rows, :], bsend.at[4], brecv.at[4], sib).wait_recv()
-
-    def piece(h, bx, by, sem, peer):
-        blk = bx * SIDE + by
-        rows = pl.ds(pl.multiple_of(blk * SLOTS, SLOTS), SLOTS)
-        ref = slots.at[h, rows, :]
-        return remote(ref, ref, ssend.at[h, sem], srecv.at[h, blk], peer)
-
-    for d in range(1, SIDE):
-        piece(0, x, y, d, at((x + d) % SIDE, y, z, c)).start()
-        piece(1, x, y, d, at(x, (y + d) % SIDE, z, c)).start()
-    for m in range(SIDE):
-        xx, yy = (x + m) % SIDE, (y + m) % SIDE
-        if m:
-            piece(0, xx, y, 0, sib).wait_recv()
-        for d in range(1, SIDE):
-            piece(0, xx, y, SIDE * (m + 1) + d, at(x, (y + d) % SIDE, z, c)).start()
-        if m:
-            piece(1, x, yy, 0, sib).wait_recv()
-        for d in range(1, SIDE):
-            piece(1, x, yy, SIDE * (m + 1) + d, at((x + d) % SIDE, y, z, c)).start()
-    for m in range(SIDE):
-        xx, yy = (x + m) % SIDE, (y + m) % SIDE
-        for d in range(1, SIDE):
-            piece(0, xx, (y + d) % SIDE, 0, sib).wait_recv()
-            piece(1, (x + d) % SIDE, yy, 0, sib).wait_recv()
-
-    wg_copy.wait()
-    wu_copy.wait()
+    lane = lax.broadcasted_iota(jnp.int32, (8, EXTRA), 1)
+    ones = jnp.where(lane < 3, 1.0, 0.0).astype(BF)
     for n in range(2):
         rows = pl.ds(n * 256, 256)
-        gate = dot(wgb[:, :half], slots[0, rows, :], NT) + dot(wgb[:, half:], slots[1, rows, :], NT)
-        up = dot(wub[:, :half], slots[0, rows, :], NT) + dot(wub[:, half:], slots[1, rows, :], NT)
-        hid_ref[0, :, rows] = sw[0:1, rows] * (gate / (1.0 + jnp.exp(-gate))) * up
-
-    for cp in ycopies:
-        cp.wait_send()
-    for d in range(1, SIDE):
-
-        @pl.when(x + d < SIDE)
-        def _():
-            remote(
-                xbuf.at[x], xbuf.at[x], xsend.at[d], xrecv.at[x], at((x + d) % SIDE, y, z, c)
-            ).wait_send()
-
-    for cp in (w2_sib, res_sib, att_sib, mix_sib, pick_sib):
-        cp.wait_send()
-
-    def drain(d, _):
-        zz = (z + d) % CHIPS
-        rows = pl.ds(pl.multiple_of(zz * 16, 16), 16)
-        peer = at(x, y, zz, c)
-        remote(part.at[rows, :], rsbuf.at[own_rows, :], zsend.at[zz], zrecv.at[z], peer).wait_send()
-        remote(
-            nrm.at[own_rows, :], nrm.at[own_rows, :], gsend.at[zz], grecv.at[z], peer
-        ).wait_send()
-        return 0
-
-    lax.fori_loop(1, CHIPS, drain, 0)
-    for h in range(2):
-        for m in range(SIDE + 1):
-            for d in range(1, SIDE):
-                piece(h, x, y, SIDE * m + d, sib).wait_send()
+        extra = slots[0, pl.ds(2 * n, 2), :, :, pl.ds(half, EXTRA)].reshape(256, EXTRA)
+        scale = dot(ones, extra, NT)[0:1, :]
+        gate = gacc[:, rows] * scale
+        hid_ref[0, :, rows] = (sw[0:1, rows] * scale) * (
+            gate / (1.0 + jnp.exp(-gate)) * uacc[:, rows]
+        )
+    finish()
 
 
 def per_device(
@@ -442,7 +565,7 @@
     half = model_width // 2
     hidden = w_gate.shape[1]
     vmem = pl.BlockSpec(memory_space=pltpu.VMEM)
-    hbm = pl.BlockSpec(memory_space=pl.ANY)
+    hbm = pl.BlockSpec(memory_space=pltpu.HBM)
     dma = pltpu.SemaphoreType.DMA
     spans = CHIPS * SLOTS
     return pl.pallas_call(
@@ -451,9 +574,17 @@
             jax.ShapeDtypeStruct(residual.shape, F32),
             jax.ShapeDtypeStruct((1, hidden, spans), F32),
         ),
-        in_specs=[vmem] * 6 + [hbm] + [vmem] * 3 + [hbm] * 2,
+        in_specs=[hbm] * 12,
         out_specs=(vmem, vmem),
         scratch_shapes=[
+            pltpu.VMEM(queries.shape, BF),
+            pltpu.VMEM(queries.shape, BF),
+            pltpu.VMEM(queries.shape, BF),
+            pltpu.VMEM(log_decay.shape, F32),
+            pltpu.VMEM((1, HS), F32),
+            pltpu.VMEM((1, model_width), F32),
+            pltpu.VMEM((2, 2, CHIPS * LC), jnp.int32),
+            pltpu.VMEM((2, 2, CHIPS * LC), F32),
             pltpu.VMEM((SIDE, ST, HS), F32),
             pltpu.VMEM((SIDE, ST, HS), F32),
             pltpu.VMEM((ST, HS), F32),
@@ -463,39 +594,44 @@
             pltpu.VMEM((2 * LC, 2 * HS), BF),
             pltpu.VMEM((2 * HS, half), BF),
             pltpu.VMEM((2 * LC, half), BF),
-            pltpu.VMEM((16, half), F32),
-            pltpu.VMEM((2 * LC, half), BF),
+            pltpu.VMEM((2 * LC, half), F32),
+            pltpu.VMEM((len(OFFS), 16, half), BF),
+            pltpu.VMEM((len(RELAYS), 16, half), BF),
             pltpu.VMEM((2,) + residual.shape, BF),
             pltpu.VMEM((16, half), F32),
             pltpu.VMEM((2, 16, half), F32),
-            pltpu.VMEM((2 * LC, half), BF),
+            pltpu.VMEM((2 * LC, half + EXTRA), BF),
             pltpu.VMEM((4, CHIPS, LC), jnp.int32),
             pltpu.VMEM((4, CHIPS, LC), F32),
             pltpu.VMEM((2 * SLOTS, 2 * LC), BF),
-            pltpu.VMEM((2, spans, half), BF),
-            pltpu.VMEM((SLOTS, half), BF),
+            pltpu.VMEM((2, SIDE, SIDE, SLOTS, half + EXTRA), BF),
+            pltpu.VMEM((SLOTS, half + EXTRA), BF),
             pltpu.VMEM((8, spans), F32),
             pltpu.VMEM((hidden, model_width), BF),
             pltpu.VMEM((hidden, model_width), BF),
-            dma((3,)),
+            pltpu.VMEM((hidden, spans), F32),
+            pltpu.VMEM((hidden, spans), F32),
+            dma((12,)),
             dma((SIDE,)),
             dma((SIDE,)),
             dma((SIDE,)),
             dma((SIDE,)),
             dma((5,)),
             dma((5,)),
-            dma((CHIPS,)),
-            dma((CHIPS,)),
-            dma((CHIPS,)),
-            dma((CHIPS,)),
-            dma((2, SIDE * (SIDE + 1) + SIDE)),
-            dma((2, CHIPS)),
+            dma((len(OFFS), PARTS)),
+            dma((len(OFFS), PARTS)),
+            dma((len(OFFS), PARTS)),
+            dma((len(OFFS), PARTS)),
+            dma((PARTS,)),
+            dma((PARTS,)),
+            dma((2, PARTS, 4, 2)),
+            dma((2, PARTS, 4, 2)),
         ],
         compiler_params=pltpu.CompilerParams(
             collective_id=0, has_side_effects=True, vmem_limit_bytes=48 << 20
         ),
         name="layer",
-    )(
+    )(*[pltpu.with_memory_space_constraint(a, pltpu.HBM) for a in (
         queries,
         key_vecs,
         value_vecs,
@@ -508,7 +644,7 @@
         jnp.transpose(route_weight, (1, 2, 0)),
         w_gate,
         w_up,
-    )
+    )])
 
 
 def solution(mesh):

time: 150 us -> 107 us (0.71)
  the two profiles are of different devices: /device:TPU:1 before, /device:TPU:32 now
where the time goes in v2:
time: 107 us
  Pallas kernels  105 us (98%)
  local copies, waits for them, and re-layouts  1.46 us (1%)
    pallas_call x1, Pallas kernels, per_device(): pl.pallas_call(kernel, out_shape=(jax.ShapeDtypeStruct(residual.shape, F3...  105 us

profile of v2, /device:TPU:32, one launch (start us, length us, event | category | flops | bytes accessed | tf_op | source)
XLA Modules:
  0.0 107.0 jit_solution(16324685381449013445)
XLA Ops:
  0.6 104.9 %layer.1 = (f32[4,2,3072]{2,1,0:T(2,128)S(1)}, f32[1,288,512]{2,1,0:T(8,128)S(1)}) custom-call(bf16[2,128,128]{2,1,0:T(8,128)(2,1)} %q_hbm.1, bf16[2,128,128]{2,1,0:T(8,128)(2,1)} %k_hbm.1, bf16[2,128,128]{2,1,0:T(8,128)(2,1)} %v_hbm.1, f32[2,1,128]{2,1,0:T(1,128)} %ld_hbm.1, f32[1,128]{1,0:T(1,128)} %bitcast.7, bf16[4,2,3072]{2,1,0:T(2,128)(2,1)} %res_hbm.1, ...), custom_call_target="tpu_custom_call" | custom-call | tf_op jit(solution)/shard_map/layer/pallas_call | solution.py:571
  105.5 0.6 copy.16
  106.2 0.8 copy.17

commit v3 on v2

--- a/solution.py
+++ b/solution.py
@@ -12,21 +12,29 @@
 F32 = jnp.float32
 SIDE = 4
 CHIPS = 16
+BLOCKS = SIDE * SIDE
+SHARE = 16
 LC = 128
 HS = 128
 SLOTS = 32
 PARTS = 3
 EXTRA = 128
 PARENT = {
-    1: 0, 3: 0, 6: 0, 2: 3, 4: 3, 5: 6, 7: 6, 8: 6,
-    -1: 0, -3: 0, -6: 0, -2: -3, -4: -3, -5: -6, -7: -6,
+    1: 0, 3: 0, 6: 3, 2: 3, 4: 3, 5: 6, 7: 6, 8: 6,
+    -1: 0, -3: 0, -6: -3, -2: -3, -4: -3, -5: -6, -7: -6,
 }
 OFFS = list(PARENT)
-CHILDREN = {p: [o for o in OFFS if PARENT[o] == p] for p in (0, 3, 6, -3, -6)}
+CHILDREN = {p: [o for o in OFFS if PARENT[o] == p] for p in set(PARENT.values())}
 LEAVES = [o for o in OFFS if o not in CHILDREN]
 RELAYS = [o for o in OFFS if o in CHILDREN]
+
+
+def depth_of(o):
+    return 0 if o == 0 else 1 + depth_of(PARENT[o])
+
+
+DEPTH = max(depth_of(o) for o in RELAYS)
 REACH = sorted({PARENT[o] - o for o in OFFS} | {o - PARENT[o] for o in OFFS})
-ST = 2 * HS + 8
 
 
 def dot(a, b, dims):
@@ -72,9 +80,9 @@
     ng_ref,
     rt_ref,
     wt_ref,
-    ybuf,
-    xbuf,
-    prefix,
+    out1,
+    in1,
+    out2,
     inc,
     inner,
     grow,
@@ -99,8 +107,8 @@
     gacc,
     uacc,
     lsem,
-    ysend,
-    yrecv,
+    asend,
+    arecv,
     xsend,
     xrecv,
     bsend,
@@ -134,14 +142,6 @@
 
     def greet(peer):
         pl.semaphore_signal(barrier, inc=1, device_id=peer, device_id_type=MESH)
-
-    greet(sib)
-    for d in range(1, SIDE):
-        greet(at(x, (y + d) % SIDE, z, c))
-        greet(at((x + d) % SIDE, y, z, c))
-
-    for d in REACH:
-        greet(at(x, y, (z + d) % CHIPS, c))
 
     mine = pl.ds(pl.multiple_of(c * half, half), half)
     theirs = pl.ds(pl.multiple_of((1 - c) * half, half), half)
@@ -170,6 +170,16 @@
     w2_own.start()
     wg_copy.start()
     wu_copy.start()
+    greet(sib)
+
+    def greet_xy(d, _):
+        greet(((s + d) % BLOCKS, e))
+        return 0
+
+    lax.fori_loop(1, BLOCKS, greet_xy, 0)
+    for d in REACH:
+        greet(at(x, y, (z + d) % CHIPS, c))
+
     for cp in ins[:3]:
         cp.wait()
 
@@ -187,18 +197,34 @@
         kw = k_ref[b].astype(F32) * jnp.exp(total - rc)
         hi, lo = split(kw)
         vb = v_ref[b]
-        ybuf[y, pl.ds(b * HS, HS), :] = dot(hi, vb, TN) + dot(lo, vb, TN)
-        ybuf[y, pl.ds(2 * HS + b, 1), :] = jnp.broadcast_to(total, (1, HS))
-    ybuf[y, pl.ds(2 * HS + 2, 6), :] = jnp.zeros((6, HS), F32)
-
-    pl.semaphore_wait(barrier, 2 * (SIDE - 1) + 1 + len(REACH))
-
-    for d in range(1, SIDE):
-        cp = remote(
-            ybuf.at[y], ybuf.at[y], ysend.at[d], yrecv.at[y], at(x, (y + d) % SIDE, z, c)
-        )
-        cp.start()
-        drains.append(cp.wait_send)
+        fresh = dot(hi, vb, TN) + dot(lo, vb, TN)
+        lines = jnp.broadcast_to(total, (8, HS))
+        for i in range(HS // SHARE):
+            j = b * (HS // SHARE) + i
+            out1[j, pl.ds(0, SHARE), :] = fresh[i * SHARE : (i + 1) * SHARE]
+            out1[j, pl.ds(SHARE, 8), :] = lines
+
+    pl.semaphore_wait(barrier, BLOCKS + len(REACH))
+
+    def order(i):
+        return BLOCKS // 2 + ((i + 1) // 2) * (1 - 2 * (i % 2))
+
+    def first(j):
+        return remote(out1.at[j], in1.at[s], asend.at[j], arecv.at[s], (j, e))
+
+    def second(j):
+        return remote(out2.at[j], inc.at[s], xsend.at[j], xrecv.at[s], (j, e))
+
+    def loop(body, start=1):
+        def turn(i, _):
+            body((s + (order(i) if start == 0 else i)) % BLOCKS)
+            return 0
+
+        lax.fori_loop(start, BLOCKS - 1 + start, turn, 0)
+
+    loop(lambda j: first(j).start(), 0)
+    drains.append(lambda: loop(lambda j: first(j).wait_send()))
+    in1[s] = out1[s]
     w2_sib = remote(outp_ref.at[:, theirs], w2.at[own_k, :], bsend.at[0], brecv.at[0], sib)
     w2_sib.start()
     drains.append(w2_sib.wait_send)
@@ -216,46 +242,15 @@
         inner[b] = dot(hi, vb, NN) + dot(lo, vb, NN)
         grow[b] = jnp.broadcast_to(jnp.exp(rc), (LC, HS))
 
-    for d in range(1, SIDE):
-        yy = (y + d) % SIDE
-        remote(
-            ybuf.at[yy], ybuf.at[yy], ysend.at[d], yrecv.at[yy], at(x, yy, z, c)
-        ).wait_recv()
-    for b in range(2):
-        rows = pl.ds(b * HS, HS)
-        run = jnp.zeros((HS, HS), F32)
-        logs = jnp.zeros((1, HS), F32)
-        pre = jnp.zeros((HS, HS), F32)
-        prelog = jnp.zeros((1, HS), F32)
-        for i in range(SIDE):
-            pre = jnp.where(y == i, run, pre)
-            prelog = jnp.where(y == i, logs, prelog)
-            tot = ybuf[i, pl.ds(2 * HS + b, 1), :]
-            run = jnp.exp(tot) * run + ybuf[i, rows, :]
-            logs = logs + tot
-        prefix[rows, :] = pre
-        prefix[pl.ds(2 * HS + b, 1), :] = prelog
-        xbuf[x, rows, :] = run
-        xbuf[x, pl.ds(2 * HS + b, 1), :] = logs
-    xbuf[x, pl.ds(2 * HS + 2, 6), :] = jnp.zeros((6, HS), F32)
-    for d in range(1, SIDE):
-
-        @pl.when(x + d < SIDE)
-        def _():
-            remote(
-                xbuf.at[x], xbuf.at[x], xsend.at[d], xrecv.at[x], at((x + d) % SIDE, y, z, c)
-            ).start()
-
-    def drain_x():
-        for d in range(1, SIDE):
-
-            @pl.when(x + d < SIDE)
-            def _():
-                remote(
-                    xbuf.at[x], xbuf.at[x], xsend.at[d], xrecv.at[x], at((x + d) % SIDE, y, z, c)
-                ).wait_send()
-
-    drains.append(drain_x)
+    loop(lambda j: remote(in1.at[j], in1.at[j], asend.at[j], arecv.at[j], (j, e)).wait_recv())
+    run = jnp.zeros((SHARE, HS), F32)
+    for j in range(BLOCKS):
+        out2[j] = run
+        keep = jnp.exp(in1[j, pl.ds(SHARE, 8), :])
+        run = jnp.concatenate([keep] * (SHARE // 8), axis=0) * run + in1[j, pl.ds(0, SHARE), :]
+    loop(lambda j: second(j).start(), 0)
+    drains.append(lambda: loop(lambda j: second(j).wait_send()))
+    inc[s] = out2[s]
 
     for b in range(2):
         for kk in range(2):
@@ -308,23 +303,10 @@
             acc = acc + (dot(hi, one, NT) + (dot(mid, one, NT) + dot(low, one, NT)))
         sw[:, pl.ds(blk * SLOTS, SLOTS)] = acc
 
-    inc[...] = jnp.zeros_like(inc)
-    for i in range(SIDE - 1):
-
-        @pl.when(x > i)
-        def _():
-            remote(
-                xbuf.at[i], xbuf.at[i], xsend.at[0], xrecv.at[i], at(i, y, z, c)
-            ).wait_recv()
-            for b in range(2):
-                rows = pl.ds(b * HS, HS)
-                tot = xbuf[i, pl.ds(2 * HS + b, 1), :]
-                inc[rows, :] = jnp.exp(tot) * inc[rows, :] + xbuf[i, rows, :]
-
+    loop(lambda j: remote(inc.at[j], inc.at[j], xsend.at[j], xrecv.at[j], (j, e)).wait_recv())
     heads = []
     for b in range(2):
-        rows = pl.ds(b * HS, HS)
-        state = prefix[rows, :] + jnp.exp(prefix[pl.ds(2 * HS + b, 1), :]) * inc[rows, :]
+        state = inc[pl.ds(b * (HS // SHARE), HS // SHARE)].reshape(HS, HS)
         hi, lo = split(state)
         qb = q_ref[b]
         raw = inner[b] + grow[b] * (dot(qb, hi, NN) + dot(qb, lo, NN))
@@ -374,9 +356,11 @@
         for o in LEAVES:
             send(rs_copy(o, p, part.at[rows_of(z - o), cols]))
 
-    def relay(p):
+    def relay(level, p):
         cols = pl.ds(p * width, width)
         for o in RELAYS:
+            if depth_of(o) != level:
+                continue
             acc = full[rows_of(z - o), cols]
             for ch in CHILDREN[o]:
                 acc = acc + rs_arrived(ch, p)
@@ -417,8 +401,10 @@
         for o in CHILDREN[0]:
             send(ag_copy(o, p, z, at(x, y, (z + o) % CHIPS, c)))
 
-    def forward(p):
+    def forward(level, p):
         for o in RELAYS:
+            if depth_of(o) != level:
+                continue
             ag_copy(o, p, z - o, sib).wait_recv()
             for ch in CHILDREN[o]:
                 send(ag_copy(ch, p, z - o, at(x, y, (z - o + ch) % CHIPS, c)))
@@ -522,11 +508,12 @@
                 res16[pl.ds(b * 8 + cc * 4 + i, 1), :] = two[b : b + 1, :]
     for p in range(PARTS):
         project(p)
-    stages = [relay, total, forward, pick, hop1, hop2, hop3, hop4, multiply]
-    for t in range(len(stages) + PARTS - 1):
+    stages = [functools.partial(relay, n) for n in range(DEPTH, 0, -1)] + [total]
+    stages += [functools.partial(forward, n) for n in range(1, DEPTH + 1)]
+    stages += [pick, hop1, hop2, hop3, hop4, multiply]
+    for stage in stages:
         for p in range(PARTS):
-            if 0 <= t - p < len(stages):
-                stages[t - p](p)
+            stage(p)
 
     for h in range(2):
         for b in range(2):
@@ -585,10 +572,10 @@
             pltpu.VMEM((1, model_width), F32),
             pltpu.VMEM((2, 2, CHIPS * LC), jnp.int32),
             pltpu.VMEM((2, 2, CHIPS * LC), F32),
-            pltpu.VMEM((SIDE, ST, HS), F32),
-            pltpu.VMEM((SIDE, ST, HS), F32),
-            pltpu.VMEM((ST, HS), F32),
-            pltpu.VMEM((2 * HS, HS), F32),
+            pltpu.VMEM((BLOCKS, SHARE + 8, HS), F32),
+            pltpu.VMEM((BLOCKS, SHARE + 8, HS), F32),
+            pltpu.VMEM((BLOCKS, SHARE, HS), F32),
+            pltpu.VMEM((BLOCKS, SHARE, HS), F32),
             pltpu.VMEM((2, LC, HS), F32),
             pltpu.VMEM((2, LC, HS), F32),
             pltpu.VMEM((2 * LC, 2 * HS), BF),
@@ -612,10 +599,10 @@
             pltpu.VMEM((hidden, spans), F32),
             pltpu.VMEM((hidden, spans), F32),
             dma((12,)),
-            dma((SIDE,)),
-            dma((SIDE,)),
-            dma((SIDE,)),
-            dma((SIDE,)),
+            dma((BLOCKS,)),
+            dma((BLOCKS,)),
+            dma((BLOCKS,)),
+            dma((BLOCKS,)),
             dma((5,)),
             dma((5,)),
             dma((len(OFFS), PARTS)),

time: 107 us -> 89.6 us (0.84)
  the two profiles are of different devices: /device:TPU:32 before, /device:TPU:1 now
where the time goes in v3:
time: 89.6 us; the launch traced here: 88.2 us
  Pallas kernels  86.1 us (96%)
  local copies, waits for them, and re-layouts  1.46 us (2%)
    pallas_call x1, Pallas kernels, per_device(): pl.pallas_call(kernel, out_shape=(jax.ShapeDtypeStruct(residual.shape, F3...  86.1 us

profile of v3, /device:TPU:1, one launch (start us, length us, event | category | flops | bytes accessed | tf_op | source)
XLA Modules:
  0.0 88.2 jit_solution(15706024922073958161)
XLA Ops:
  0.6 86.1 %layer.1 = (f32[4,2,3072]{2,1,0:T(2,128)S(1)}, f32[1,288,512]{2,1,0:T(8,128)S(1)}) custom-call(bf16[2,128,128]{2,1,0:T(8,128)(2,1)} %q_hbm.1, bf16[2,128,128]{2,1,0:T(8,128)(2,1)} %k_hbm.1, bf16[2,128,128]{2,1,0:T(8,128)(2,1)} %v_hbm.1, f32[2,1,128]{2,1,0:T(1,128)} %ld_hbm.1, f32[1,128]{1,0:T(1,128)} %bitcast.7, bf16[4,2,3072]{2,1,0:T(2,128)(2,1)} %res_hbm.1, ...), custom_call_target="tpu_custom_call" | custom-call | tf_op jit(solution)/shard_map/layer/pallas_call | solution.py:558
  86.7 0.6 copy.16
  87.4 0.8 copy.17

commit v4 on v3

--- a/solution.py
+++ b/solution.py
@@ -102,10 +102,8 @@
     slots,
     other,
     sw,
-    wgb,
-    wub,
-    gacc,
-    uacc,
+    wb,
+    acc2,
     lsem,
     asend,
     arecv,
@@ -127,6 +125,7 @@
     x, y, z, c = s // SIDE, s % SIDE, e // 2, e % 2
     half = mix.shape[2]
     depth = 2 * half
+    hidden = wg_ref.shape[1]
 
     drains = []
 
@@ -147,8 +146,8 @@
     theirs = pl.ds(pl.multiple_of((1 - c) * half, half), half)
     own_k = pl.ds(pl.multiple_of(c * HS, HS), HS)
     w2_own = pltpu.make_async_copy(outp_ref.at[:, mine], w2.at[own_k, :], lsem.at[0])
-    wg_copy = pltpu.make_async_copy(wg_ref.at[0], wgb, lsem.at[1])
-    wu_copy = pltpu.make_async_copy(wu_ref.at[0], wub, lsem.at[2])
+    wg_copy = pltpu.make_async_copy(wg_ref.at[0], wb.at[pl.ds(0, hidden), :], lsem.at[1])
+    wu_copy = pltpu.make_async_copy(wu_ref.at[0], wb.at[pl.ds(hidden, hidden), :], lsem.at[2])
     ins = [
         pltpu.make_async_copy(a, b, lsem.at[3 + i])
         for i, (a, b) in enumerate(
@@ -353,8 +352,12 @@
         got = dot(att[...], w2[:, cols], NN)
         full[:, cols] = got
         part[:, cols] = got.astype(BF)
+
+    def leaves(level, p):
+        cols = pl.ds(p * width, width)
         for o in LEAVES:
-            send(rs_copy(o, p, part.at[rows_of(z - o), cols]))
+            if depth_of(o) == level:
+                send(rs_copy(o, p, part.at[rows_of(z - o), cols]))
 
     def relay(level, p):
         cols = pl.ds(p * width, width)
@@ -398,31 +401,32 @@
                 lane == 0, hi, jnp.where(lane == 1, mid, jnp.where(lane == 2, low, 0.0))
             )
             nrm[own_rows, pl.ds(half, EXTRA)] = extra.astype(BF)
-        for o in CHILDREN[0]:
-            send(ag_copy(o, p, z, at(x, y, (z + o) % CHIPS, c)))
+        spread(0, RELAYS, p)
+
+    def spread(level, which, p):
+        for o in OFFS:
+            src = z - PARENT[o]
+            if depth_of(PARENT[o]) == level and o in which:
+                send(ag_copy(o, p, src, at(x, y, (src + o) % CHIPS, c)))
 
     def forward(level, p):
         for o in RELAYS:
-            if depth_of(o) != level:
-                continue
-            ag_copy(o, p, z - o, sib).wait_recv()
-            for ch in CHILDREN[o]:
-                send(ag_copy(ch, p, z - o, at(x, y, (z - o + ch) % CHIPS, c)))
-
-    theirs_p = pl.ds(pl.multiple_of((1 - c) * SLOTS, SLOTS), SLOTS)
-    mine_p = pl.ds(pl.multiple_of(c * SLOTS, SLOTS), SLOTS)
+            if depth_of(o) == level:
+                ag_copy(o, p, z - o, sib).wait_recv()
+        spread(level, RELAYS, p)
 
     def pick(p):
         for o in LEAVES:
             ag_copy(o, p, z - o, sib).wait_recv()
         cols = span(p)
-        other[:, cols] = dot(picks[theirs_p, :], nrm[:, cols], NN).astype(BF)
+        got = dot(picks[...], nrm[:, cols], NN).astype(BF)
+        other[:, cols] = jnp.where(c == 0, got[SLOTS:], got[:SLOTS])
         send(
             remote(
                 other.at[:, cols], slots.at[c, x, y, :, cols], psend.at[p], precv.at[p], sib
             )
         )
-        slots[c, x, y, :, cols] = dot(picks[mine_p, :], nrm[:, cols], NN).astype(BF)
+        slots[c, x, y, :, cols] = jnp.where(c == 0, got[:SLOTS], got[SLOTS:])
 
     def parts_of(p):
         size = width + (EXTRA if p == PARTS - 1 else 0)
@@ -456,21 +460,14 @@
             other.at[:, cols], slots.at[1 - c, x, y, :, cols], psend.at[p], precv.at[p], sib
         ).wait_recv()
         for h in range(2):
-            for i, d in enumerate((1, -1)):
+            for i, d in reversed(list(enumerate((1, -1, 2)))):
                 send(xy(h, p, 0, i, one(h, (x, y), cols), step1(h, d)))
 
-    def hop2(p):
+    def hop3(p):
         for h in range(2):
-            for i, d in enumerate((1, -1)):
+            for i, d in enumerate((1, -1, 2)):
                 back = step1(h, -d)
                 xy(h, p, 0, i, one(h, back, span(p)), back).wait_recv()
-                send(xy(h, p, 1, i, one(h, back, parts_of(p)[i]), step1(h, d)))
-
-    def hop3(p):
-        for h in range(2):
-            for i, d in enumerate((1, -1)):
-                far = step1(h, 2)
-                xy(h, p, 1, i, one(h, far, parts_of(p)[i]), far).wait_recv()
             for i, d in enumerate((1, -1)):
                 send(xy(h, p, 2, i, four(h, (x, y), span(p)), step2(h, d)))
 
@@ -491,14 +488,13 @@
             wu_copy.wait()
         for n in range(2):
             rows = pl.ds(n * 256, 256)
-            for w, acc in ((wgb, gacc), (wub, uacc)):
-                got = None
-                for h in range(2):
-                    rhs = slots[h, pl.ds(2 * n, 2), :, :, pl.ds(p * width, width)]
-                    rhs = rhs.reshape(256, width)
-                    term = dot(w[:, pl.ds(h * half + p * width, width)], rhs, NT)
-                    got = term if got is None else got + term
-                acc[:, rows] = got if p == 0 else acc[:, rows] + got
+            got = None
+            for h in range(2):
+                rhs = slots[h, pl.ds(2 * n, 2), :, :, pl.ds(p * width, width)]
+                rhs = rhs.reshape(256, width)
+                term = dot(wb[:, pl.ds(h * half + p * width, width)], rhs, NT)
+                got = term if got is None else got + term
+            acc2[:, rows] = got if p == 0 else acc2[:, rows] + got
 
     remote(res_hbm, resbuf.at[1 - c], bsend.at[1], brecv.at[1], sib).wait_recv()
     for cc in range(2):
@@ -506,14 +502,32 @@
             two = resbuf[cc, i, :, mine].astype(F32)
             for b in range(2):
                 res16[pl.ds(b * 8 + cc * 4 + i, 1), :] = two[b : b + 1, :]
-    for p in range(PARTS):
-        project(p)
-    stages = [functools.partial(relay, n) for n in range(DEPTH, 0, -1)] + [total]
-    stages += [functools.partial(forward, n) for n in range(1, DEPTH + 1)]
-    stages += [pick, hop1, hop2, hop3, hop4, multiply]
-    for stage in stages:
+    def each(*steps):
         for p in range(PARTS):
-            stage(p)
+            for step in steps:
+                step(p)
+
+    def leaf(level):
+        return functools.partial(leaves, level)
+
+    def near(level):
+        return functools.partial(spread, level, LEAVES)
+
+    each(project, leaf(DEPTH + 1))
+    for level in range(DEPTH, 0, -1):
+        each(leaf(level))
+        each(functools.partial(relay, level))
+    each(total, near(0))
+    for level in range(1, DEPTH + 1):
+        each(functools.partial(forward, level), near(level))
+    pick(0)
+    for p in range(1, PARTS):
+        pick(p)
+        hop1(p - 1)
+    hop1(PARTS - 1)
+    each(hop3)
+    each(hop4)
+    each(multiply)
 
     for h in range(2):
         for b in range(2):
@@ -527,9 +541,9 @@
         rows = pl.ds(n * 256, 256)
         extra = slots[0, pl.ds(2 * n, 2), :, :, pl.ds(half, EXTRA)].reshape(256, EXTRA)
         scale = dot(ones, extra, NT)[0:1, :]
-        gate = gacc[:, rows] * scale
+        gate = acc2[pl.ds(0, hidden), rows] * scale
         hid_ref[0, :, rows] = (sw[0:1, rows] * scale) * (
-            gate / (1.0 + jnp.exp(-gate)) * uacc[:, rows]
+            gate / (1.0 + jnp.exp(-gate)) * acc2[pl.ds(hidden, hidden), rows]
         )
     finish()
 
@@ -594,10 +608,8 @@
             pltpu.VMEM((2, SIDE, SIDE, SLOTS, half + EXTRA), BF),
             pltpu.VMEM((SLOTS, half + EXTRA), BF),
             pltpu.VMEM((8, spans), F32),
-            pltpu.VMEM((hidden, model_width), BF),
-            pltpu.VMEM((hidden, model_width), BF),
-            pltpu.VMEM((hidden, spans), F32),
-            pltpu.VMEM((hidden, spans), F32),
+            pltpu.VMEM((2 * hidden, model_width), BF),
+            pltpu.VMEM((2 * hidden, spans), F32),
             dma((12,)),
             dma((BLOCKS,)),
             dma((BLOCKS,)),
@@ -611,8 +623,8 @@
             dma((len(OFFS), PARTS)),
             dma((PARTS,)),
             dma((PARTS,)),
-            dma((2, PARTS, 4, 2)),
-            dma((2, PARTS, 4, 2)),
+            dma((2, PARTS, 4, 3)),
+            dma((2, PARTS, 4, 3)),
         ],
         compiler_params=pltpu.CompilerParams(
             collective_id=0, has_side_effects=True, vmem_limit_bytes=48 << 20

time: 89.6 us -> 86.6 us (0.967); the launches traced: 88.2 us -> 86.5 us
  Pallas kernels: 86.1 us -> 84.4 us
    pallas_call x1, Pallas kernels: 86.1 us -> 84.4 us  [per_device(): pl.pallas_call(kernel, out_shape=(jax.ShapeDtypeStruct(residual.shape, F3...]
where the time goes in v4:
time: 86.6 us; the launch traced here: 86.5 us
  Pallas kernels  84.4 us (97%)
  local copies, waits for them, and re-layouts  1.46 us (2%)
    pallas_call x1, Pallas kernels, per_device(): pl.pallas_call(kernel, out_shape=(jax.ShapeDtypeStruct(residual.shape, F3...  84.4 us

profile of v4, /device:TPU:1, one launch (start us, length us, event | category | flops | bytes accessed | tf_op | source)
XLA Modules:
  0.0 86.5 jit_solution(4843061197146200502)
XLA Ops:
  0.6 84.4 %layer.1 = (f32[4,2,3072]{2,1,0:T(2,128)S(1)}, f32[1,288,512]{2,1,0:T(8,128)S(1)}) custom-call(bf16[2,128,128]{2,1,0:T(8,128)(2,1)} %q_hbm.1, bf16[2,128,128]{2,1,0:T(8,128)(2,1)} %k_hbm.1, bf16[2,128,128]{2,1,0:T(8,128)(2,1)} %v_hbm.1, f32[2,1,128]{2,1,0:T(1,128)} %ld_hbm.1, f32[1,128]{1,0:T(1,128)} %bitcast.7, bf16[4,2,3072]{2,1,0:T(2,128)(2,1)} %res_hbm.1, ...), custom_call_target="tpu_custom_call" | custom-call | tf_op jit(solution)/shard_map/layer/pallas_call | solution.py:572
  85.0 0.6 copy.16
  85.6 0.8 copy.17

commit v5 on v4

--- a/solution.py
+++ b/solution.py
@@ -21,7 +21,7 @@
 EXTRA = 128
 PARENT = {
     1: 0, 3: 0, 6: 3, 2: 3, 4: 3, 5: 6, 7: 6, 8: 6,
-    -1: 0, -3: 0, -6: -3, -2: -3, -4: -3, -5: -6, -7: -6,
+    -1: 0, -2: 0, -5: -2, -3: -2, -4: -5, -6: -5, -7: -5,
 }
 OFFS = list(PARENT)
 CHILDREN = {p: [o for o in OFFS if PARENT[o] == p] for p in set(PARENT.values())}

time: 86.6 us -> 85.3 us (0.985)
  Pallas kernels: 84.4 us -> 83.1 us
    pallas_call x1, Pallas kernels: 84.4 us -> 83.1 us  [per_device(): pl.pallas_call(kernel, out_shape=(jax.ShapeDtypeStruct(residual.shape, F3...]
where the time goes in v5:
time: 85.3 us; the launch traced here: 85.2 us
  Pallas kernels  83.1 us (97%)
  local copies, waits for them, and re-layouts  1.46 us (2%)
    pallas_call x1, Pallas kernels, per_device(): pl.pallas_call(kernel, out_shape=(jax.ShapeDtypeStruct(residual.shape, F3...  83.1 us

profile of v5, /device:TPU:1, one launch (start us, length us, event | category | flops | bytes accessed | tf_op | source)
XLA Modules:
  0.0 85.2 jit_solution(11069528123879318659)
XLA Ops:
  0.6 83.1 %layer.1 = (f32[4,2,3072]{2,1,0:T(2,128)S(1)}, f32[1,288,512]{2,1,0:T(8,128)S(1)}) custom-call(bf16[2,128,128]{2,1,0:T(8,128)(2,1)} %q_hbm.1, bf16[2,128,128]{2,1,0:T(8,128)(2,1)} %k_hbm.1, bf16[2,128,128]{2,1,0:T(8,128)(2,1)} %v_hbm.1, f32[2,1,128]{2,1,0:T(1,128)} %ld_hbm.1, f32[1,128]{1,0:T(1,128)} %bitcast.7, bf16[4,2,3072]{2,1,0:T(2,128)(2,1)} %res_hbm.1, ...), custom_call_target="tpu_custom_call" | custom-call | tf_op jit(solution)/shard_map/layer/pallas_call | solution.py:572
  83.7 0.6 copy.16
  84.4 0.8 copy.17
